TPU v7x, 32 devices: a whole 2x2x4 slice. The times are simulated.
32 devices in a mesh: energy: 4 (over y, x), slab: 8 (over z, core).
Axes of the slice: x: 2, y: 2, z: 4, core: 2. Of those that a mesh axis runs over, the one named last changes fastest.
Arguments:
- left_basis: bfloat16 [8, 768, 768], P('slab'), may hold values from -0.21875 to 0.21875
- right_basis: bfloat16 [8, 768, 768], P('slab'), may hold values from -0.21875 to 0.21875
- potential_index: int32 [8], P('slab'), may hold values from 0 to 7
- levels: float32 [8, 768], replicated, may hold values from 0.8 to 1.25
- energy_values: float32 [64], replicated, may hold values from -0.1 to 0.1
- energy_weights: float32 [64], replicated, may hold values from 0.2 to 5
- energy_index: int32 [16], P('energy'), may hold values from 0 to 63
- left_source: bfloat16 [768, 128], replicated, may hold values from -6 to 6
- right_source: bfloat16 [768, 128], replicated, may hold values from -6 to 6
Outputs:
- density: float32 [8, 768], P('slab')
All inputs are finite; a program needn't handle non-finite values.
Results may differ from a plain program's by a relative error of at most 0.0044.
Values may be sent and summed in bfloat16 or wider, within the bound.
A program may use at most 64 MiB of HBM per device.

v0:
```python
import jax
import jax.numpy as jnp
from jax import lax
from jax.sharding import PartitionSpec as P


def passed_along(block, axis, distance):
    devices = range(lax.axis_size(axis))
    route = [(i - distance, i) for i in devices if i - distance in devices]
    return lax.ppermute(block, axis, route)


def local(
    left_basis,
    right_basis,
    potential_index,
    levels,
    energy_values,
    energy_weights,
    energy_index,
    left_source,
    right_source,
):
    slab_count = left_basis.shape[0]
    energy_count = energy_index.shape[0]
    orbitals = left_basis.shape[1]
    modes = left_source.shape[1]
    chain = lax.axis_size("slab")
    position = lax.axis_index("slab")
    total_energies = energy_count * lax.axis_size("energy")
    grid_ids = jnp.arange(energy_values.shape[0], dtype=jnp.int32)
    picked = (energy_index[:, None] == grid_ids[None, :]).astype(jnp.float32)
    energy = jnp.sum(picked * energy_values[None, :], axis=1)
    weight = jnp.sum(picked * energy_weights[None, :], axis=1) / (total_energies * modes)
    profile_ids = jnp.arange(levels.shape[0], dtype=jnp.int32)
    profile = (potential_index[:, None] == profile_ids[None, :]).astype(jnp.float32)
    slab_levels = jnp.sum(profile[:, :, None] * levels[None], axis=1)
    factors_all = 1.0 / (energy[None, :, None] - slab_levels[:, None, :])
    slot_ids = jnp.arange(energy_count, dtype=jnp.int32)

    def select(slot):
        chosen = (slot_ids == slot).astype(jnp.float32)
        return (jnp.sum(chosen[None, :, None] * factors_all, axis=1), jnp.sum(chosen * weight))

    def contribution(state, scale):
        squared = state.astype(jnp.float32) ** 2
        return scale * jnp.sum(squared, axis=1)

    def sweep_down(state, factors, scale):
        mixed = jnp.dot(right_basis[0], state, preferred_element_type=jnp.float32)
        scaled = (factors[0][:, None] * mixed).astype(jnp.bfloat16)
        state = jnp.dot(left_basis[0], scaled, preferred_element_type=jnp.float32).astype(
            jnp.bfloat16
        )
        parts = [contribution(state, scale)]
        return (state, jnp.stack(parts))

    def sweep_up(state, factors, scale):
        parts = []
        for index in reversed(range(slab_count)):
            mixed = jnp.einsum(
                "wv,wm->vm", left_basis[index], state, preferred_element_type=jnp.float32
            )
            scaled = (factors[index][:, None] * mixed).astype(jnp.bfloat16)
            state = jnp.einsum(
                "wv,wm->vm", right_basis[index], scaled, preferred_element_type=jnp.float32
            ).astype(jnp.bfloat16)
            parts.append(contribution(state, scale))
        return (state, jnp.stack(parts[::-1]))

    def forward_work(turn, incoming, state, density):
        start = jnp.where(position == 0, left_source, incoming)
        slot = turn - position
        factors, scale = select(slot)
        active = (slot >= 0) & (slot < energy_count)

        def forward_run(begin):
            fresh, parts = sweep_down(begin, factors, scale)
            return (fresh, density + parts)

        def forward_rest(begin):
            return (state, density)

        return lax.cond(active, forward_run, forward_rest, start)

    def backward_work(turn, incoming, state, density):
        start = jnp.where(position == chain - 1, right_source, incoming)
        slot = turn - (chain - 1 - position)
        factors, scale = select(slot)
        active = (slot >= 0) & (slot < energy_count)

        def backward_run(begin):
            fresh, parts = sweep_up(begin, factors, scale)
            return (fresh, density + parts)

        def backward_rest(begin):
            return (state, density)

        return lax.cond(active, backward_run, backward_rest, start)

    turns = chain + energy_count - 1
    zero_state = jnp.zeros((orbitals, modes), jnp.bfloat16)
    zero_density = jnp.zeros((slab_count, orbitals), jnp.float32)

    def forward_turn(turn, carry):
        state, density = carry
        incoming = passed_along(state, "slab", 1)
        return forward_work(turn, incoming, state, density)

    def backward_turn(turn, carry):
        state, density = carry
        incoming = passed_along(state, "slab", -1)
        return backward_work(turn, incoming, state, density)

    _, forward_density = lax.fori_loop(0, turns, forward_turn, (zero_state, zero_density))
    _, backward_density = lax.fori_loop(0, turns, backward_turn, (zero_state, zero_density))
    return lax.psum(forward_density + backward_density, "energy")


def solution(mesh):
    placed = (
        P("slab", None, None),
        P("slab", None, None),
        P("slab"),
        P(),
        P(),
        P(),
        P("energy"),
        P(),
        P(),
    )
    return jax.shard_map(
        local, mesh=mesh, in_specs=placed, out_specs=P("slab", None), check_vma=False
    )
```

profile of v0, /device:TPU:24, one launch (start us, length us, event | category | flops | bytes accessed | tf_op | source)
XLA Modules:
  0.0 214.1 jit_solution(8526664352582363796)
XLA Ops:
  0.0 0.9 select_reduce_fusion.1
  2.4 93.5 %while.38 = (s32[]{:T(128)}, bf16[768,128]{0,1:T(8,128)(2,1)S(1)}, f32[1,768]{1,0:T(1,128)S(1)}, s32[]{:T(128)}, pred[]{:T(512)}, /*index=5*/bf16[768,128]{1,0:T...) while((s32[]{:T(128)}, bf16[768,128]{0,1:T(8,128)(2,1)S(1)}, ...), condition=%wide.region_16.17_spmd.clone.clone, body=%wide.region_10.16_spmd.clone.clone.sunk | while | flops 302690304 | bytes 4156900 | solution.py:116
  2.6 1.9 collective-permute-start.1
  4.6 3.2 %collective-permute-done.1 = bf16[768,128]{1,0:T(8,128)(2,1)S(1)} collective-permute-done((bf16[768,128]{1,0:T(8,128)(2,1)S(1)}, bf16[768,128]{1,0:T(8,128)(2,1)S(1)}, u32[]{:S(2)}, u32[]{:S(2)}) %collective-permute-start.1) | collective-permute-done | bytes 196640 | tf_op jit(solution)/shard_map/while/body/eval_jaxpr/ppermute | solution.py:10
  7.9 3.8 %collective-permute-start.1 = (bf16[768,128]{1,0:T(8,128)(2,1)S(1)}, bf16[768,128]{1,0:T(8,128)(2,1)S(1)}, u32[]{:S(2)}, u32[]{:S(2)}) collective-permute-start(bf16[768,128]{1,0:T(8,128)(2,1)S(1)} %copy.17), channel_id=1, source_target_pairs={{1,0},{2,1},{3,2},{4,3},{5,4},{6,5},{7,6},{9,8},{10,9},{11,10},{12... | collective-permute-start | bytes 589832 | tf_op jit(solution)/shard_map/while/body/eval_jaxpr/ppermute | solution.py:10
  11.7 3.2 %collective-permute-done.1 = bf16[768,128]{1,0:T(8,128)(2,1)S(1)} collective-permute-done((bf16[768,128]{1,0:T(8,128)(2,1)S(1)}, bf16[768,128]{1,0:T(8,128)(2,1)S(1)}, u32[]{:S(2)}, u32[]{:S(2)}) %collective-permute-start.1) | collective-permute-done | bytes 196640 | tf_op jit(solution)/shard_map/while/body/eval_jaxpr/ppermute | solution.py:10
  14.9 3.7 %conditional.9 = ((bf16[768,128]{0,1:T(8,128)(2,1)S(1)}, f32[1,768]{1,0:T(1,128)S(1)})) conditional(s32[]{:T(128)} %convert_element_type.149, (bf16[768,128]{0,1:T(8,128)(2,1)S(1)}, f32[1,768]{1,0:T(1,128)S(1)}) %tuple.128, (s32[4]{0:T(128)S(1)}, pred[]{:T(512)}, bf16[768,128]{1,0:T(8,128)(2,1)}, bf16[768,128]{1,0:T(8,128)(2,1)S(1)}, ...), branch_computations={%region_11.11_spmd, %region_12.15_spmd.clone} | conditional | flops 302690304 | bytes 2976905 | solution.py:99
  15.0 2.3 %multiply_reduce_fusion.1 = (f32[768]{0:T(1024)S(1)}, bf16[768,128]{0,1:T(8,128)(2,1)S(1)}) fusion(bf16[1,768,768]{2,1,0:T(8,128)(2,1)} %get-tuple-element.853, bf16[1,768,768]{2,1,0:T(8,128)(2,1)} %get-tuple-element.852, bf16[768,128]{1,0:T(8,128)(2,1)} %get-tuple-element.850, bf16[768,128]{1,0:T(8,128)(2,1)S(1)} %get-tuple-element.851, ...), kind=kOutput, calls=%fused_computation.30 | convolution fusion | flops 302677248 | bytes 2955265 | tf_op jit(solution)/shard_map/while/body/eval_jaxpr/cond/branch_1_fun/wv,wm->vm/dot_general | solution.py:65
  18.8 1.9 collective-permute-start.1
  20.7 3.2 %collective-permute-done.1 = bf16[768,128]{1,0:T(8,128)(2,1)S(1)} collective-permute-done((bf16[768,128]{1,0:T(8,128)(2,1)S(1)}, bf16[768,128]{1,0:T(8,128)(2,1)S(1)}, u32[]{:S(2)}, u32[]{:S(2)}) %collective-permute-start.1) | collective-permute-done | bytes 196640 | tf_op jit(solution)/shard_map/while/body/eval_jaxpr/ppermute | solution.py:10
  23.9 3.7 %conditional.9 = ((bf16[768,128]{0,1:T(8,128)(2,1)S(1)}, f32[1,768]{1,0:T(1,128)S(1)})) conditional(s32[]{:T(128)} %convert_element_type.149, (bf16[768,128]{0,1:T(8,128)(2,1)S(1)}, f32[1,768]{1,0:T(1,128)S(1)}) %tuple.128, (s32[4]{0:T(128)S(1)}, pred[]{:T(512)}, bf16[768,128]{1,0:T(8,128)(2,1)}, bf16[768,128]{1,0:T(8,128)(2,1)S(1)}, ...), branch_computations={%region_11.11_spmd, %region_12.15_spmd.clone} | conditional | flops 302690304 | bytes 2976905 | solution.py:99
  24.0 2.3 %multiply_reduce_fusion.1 = (f32[768]{0:T(1024)S(1)}, bf16[768,128]{0,1:T(8,128)(2,1)S(1)}) fusion(bf16[1,768,768]{2,1,0:T(8,128)(2,1)} %get-tuple-element.853, bf16[1,768,768]{2,1,0:T(8,128)(2,1)} %get-tuple-element.852, bf16[768,128]{1,0:T(8,128)(2,1)} %get-tuple-element.850, bf16[768,128]{1,0:T(8,128)(2,1)S(1)} %get-tuple-element.851, ...), kind=kOutput, calls=%fused_computation.30 | convolution fusion | flops 302677248 | bytes 2955265 | tf_op jit(solution)/shard_map/while/body/eval_jaxpr/cond/branch_1_fun/wv,wm->vm/dot_general | solution.py:65
  27.7 3.8 %collective-permute-start.1 = (bf16[768,128]{1,0:T(8,128)(2,1)S(1)}, bf16[768,128]{1,0:T(8,128)(2,1)S(1)}, u32[]{:S(2)}, u32[]{:S(2)}) collective-permute-start(bf16[768,128]{1,0:T(8,128)(2,1)S(1)} %copy.17), channel_id=1, source_target_pairs={{1,0},{2,1},{3,2},{4,3},{5,4},{6,5},{7,6},{9,8},{10,9},{11,10},{12... | collective-permute-start | bytes 589832 | tf_op jit(solution)/shard_map/while/body/eval_jaxpr/ppermute | solution.py:10
  31.6 3.2 %collective-permute-done.1 = bf16[768,128]{1,0:T(8,128)(2,1)S(1)} collective-permute-done((bf16[768,128]{1,0:T(8,128)(2,1)S(1)}, bf16[768,128]{1,0:T(8,128)(2,1)S(1)}, u32[]{:S(2)}, u32[]{:S(2)}) %collective-permute-start.1) | collective-permute-done | bytes 196640 | tf_op jit(solution)/shard_map/while/body/eval_jaxpr/ppermute | solution.py:10
  34.7 3.7 %conditional.9 = ((bf16[768,128]{0,1:T(8,128)(2,1)S(1)}, f32[1,768]{1,0:T(1,128)S(1)})) conditional(s32[]{:T(128)} %convert_element_type.149, (bf16[768,128]{0,1:T(8,128)(2,1)S(1)}, f32[1,768]{1,0:T(1,128)S(1)}) %tuple.128, (s32[4]{0:T(128)S(1)}, pred[]{:T(512)}, bf16[768,128]{1,0:T(8,128)(2,1)}, bf16[768,128]{1,0:T(8,128)(2,1)S(1)}, ...), branch_computations={%region_11.11_spmd, %region_12.15_spmd.clone} | conditional | flops 302690304 | bytes 2976905 | solution.py:99
  34.8 2.3 %multiply_reduce_fusion.1 = (f32[768]{0:T(1024)S(1)}, bf16[768,128]{0,1:T(8,128)(2,1)S(1)}) fusion(bf16[1,768,768]{2,1,0:T(8,128)(2,1)} %get-tuple-element.853, bf16[1,768,768]{2,1,0:T(8,128)(2,1)} %get-tuple-element.852, bf16[768,128]{1,0:T(8,128)(2,1)} %get-tuple-element.850, bf16[768,128]{1,0:T(8,128)(2,1)S(1)} %get-tuple-element.851, ...), kind=kOutput, calls=%fused_computation.30 | convolution fusion | flops 302677248 | bytes 2955265 | tf_op jit(solution)/shard_map/while/body/eval_jaxpr/cond/branch_1_fun/wv,wm->vm/dot_general | solution.py:65
  38.6 3.8 %collective-permute-start.1 = (bf16[768,128]{1,0:T(8,128)(2,1)S(1)}, bf16[768,128]{1,0:T(8,128)(2,1)S(1)}, u32[]{:S(2)}, u32[]{:S(2)}) collective-permute-start(bf16[768,128]{1,0:T(8,128)(2,1)S(1)} %copy.17), channel_id=1, source_target_pairs={{1,0},{2,1},{3,2},{4,3},{5,4},{6,5},{7,6},{9,8},{10,9},{11,10},{12... | collective-permute-start | bytes 589832 | tf_op jit(solution)/shard_map/while/body/eval_jaxpr/ppermute | solution.py:10
  42.4 3.2 %collective-permute-done.1 = bf16[768,128]{1,0:T(8,128)(2,1)S(1)} collective-permute-done((bf16[768,128]{1,0:T(8,128)(2,1)S(1)}, bf16[768,128]{1,0:T(8,128)(2,1)S(1)}, u32[]{:S(2)}, u32[]{:S(2)}) %collective-permute-start.1) | collective-permute-done | bytes 196640 | tf_op jit(solution)/shard_map/while/body/eval_jaxpr/ppermute | solution.py:10
  45.6 3.7 %conditional.9 = ((bf16[768,128]{0,1:T(8,128)(2,1)S(1)}, f32[1,768]{1,0:T(1,128)S(1)})) conditional(s32[]{:T(128)} %convert_element_type.149, (bf16[768,128]{0,1:T(8,128)(2,1)S(1)}, f32[1,768]{1,0:T(1,128)S(1)}) %tuple.128, (s32[4]{0:T(128)S(1)}, pred[]{:T(512)}, bf16[768,128]{1,0:T(8,128)(2,1)}, bf16[768,128]{1,0:T(8,128)(2,1)S(1)}, ...), branch_computations={%region_11.11_spmd, %region_12.15_spmd.clone} | conditional | flops 302690304 | bytes 2976905 | solution.py:99
  45.7 2.3 %multiply_reduce_fusion.1 = (f32[768]{0:T(1024)S(1)}, bf16[768,128]{0,1:T(8,128)(2,1)S(1)}) fusion(bf16[1,768,768]{2,1,0:T(8,128)(2,1)} %get-tuple-element.853, bf16[1,768,768]{2,1,0:T(8,128)(2,1)} %get-tuple-element.852, bf16[768,128]{1,0:T(8,128)(2,1)} %get-tuple-element.850, bf16[768,128]{1,0:T(8,128)(2,1)S(1)} %get-tuple-element.851, ...), kind=kOutput, calls=%fused_computation.30 | convolution fusion | flops 302677248 | bytes 2955265 | tf_op jit(solution)/shard_map/while/body/eval_jaxpr/cond/branch_1_fun/wv,wm->vm/dot_general | solution.py:65
  49.5 3.8 %collective-permute-start.1 = (bf16[768,128]{1,0:T(8,128)(2,1)S(1)}, bf16[768,128]{1,0:T(8,128)(2,1)S(1)}, u32[]{:S(2)}, u32[]{:S(2)}) collective-permute-start(bf16[768,128]{1,0:T(8,128)(2,1)S(1)} %copy.17), channel_id=1, source_target_pairs={{1,0},{2,1},{3,2},{4,3},{5,4},{6,5},{7,6},{9,8},{10,9},{11,10},{12... | collective-permute-start | bytes 589832 | tf_op jit(solution)/shard_map/while/body/eval_jaxpr/ppermute | solution.py:10
  53.3 3.2 %collective-permute-done.1 = bf16[768,128]{1,0:T(8,128)(2,1)S(1)} collective-permute-done((bf16[768,128]{1,0:T(8,128)(2,1)S(1)}, bf16[768,128]{1,0:T(8,128)(2,1)S(1)}, u32[]{:S(2)}, u32[]{:S(2)}) %collective-permute-start.1) | collective-permute-done | bytes 196640 | tf_op jit(solution)/shard_map/while/body/eval_jaxpr/ppermute | solution.py:10
  56.6 7.5 %collective-permute-start.1 = (bf16[768,128]{1,0:T(8,128)(2,1)S(1)}, bf16[768,128]{1,0:T(8,128)(2,1)S(1)}, u32[]{:S(2)}, u32[]{:S(2)}) collective-permute-start(bf16[768,128]{1,0:T(8,128)(2,1)S(1)} %copy.17), channel_id=1, source_target_pairs={{1,0},{2,1},{3,2},{4,3},{5,4},{6,5},{7,6},{9,8},{10,9},{11,10},{12... | collective-permute-start | bytes 589832 | tf_op jit(solution)/shard_map/while/body/eval_jaxpr/ppermute | solution.py:10
  64.2 3.2 %collective-permute-done.1 = bf16[768,128]{1,0:T(8,128)(2,1)S(1)} collective-permute-done((bf16[768,128]{1,0:T(8,128)(2,1)S(1)}, bf16[768,128]{1,0:T(8,128)(2,1)S(1)}, u32[]{:S(2)}, u32[]{:S(2)}) %collective-permute-start.1) | collective-permute-done | bytes 196640 | tf_op jit(solution)/shard_map/while/body/eval_jaxpr/ppermute | solution.py:10
  67.5 3.8 %collective-permute-start.1 = (bf16[768,128]{1,0:T(8,128)(2,1)S(1)}, bf16[768,128]{1,0:T(8,128)(2,1)S(1)}, u32[]{:S(2)}, u32[]{:S(2)}) collective-permute-start(bf16[768,128]{1,0:T(8,128)(2,1)S(1)} %copy.17), channel_id=1, source_target_pairs={{1,0},{2,1},{3,2},{4,3},{5,4},{6,5},{7,6},{9,8},{10,9},{11,10},{12... | collective-permute-start | bytes 589832 | tf_op jit(solution)/shard_map/while/body/eval_jaxpr/ppermute | solution.py:10
  71.3 3.2 %collective-permute-done.1 = bf16[768,128]{1,0:T(8,128)(2,1)S(1)} collective-permute-done((bf16[768,128]{1,0:T(8,128)(2,1)S(1)}, bf16[768,128]{1,0:T(8,128)(2,1)S(1)}, u32[]{:S(2)}, u32[]{:S(2)}) %collective-permute-start.1) | collective-permute-done | bytes 196640 | tf_op jit(solution)/shard_map/while/body/eval_jaxpr/ppermute | solution.py:10
  74.7 3.8 %collective-permute-start.1 = (bf16[768,128]{1,0:T(8,128)(2,1)S(1)}, bf16[768,128]{1,0:T(8,128)(2,1)S(1)}, u32[]{:S(2)}, u32[]{:S(2)}) collective-permute-start(bf16[768,128]{1,0:T(8,128)(2,1)S(1)} %copy.17), channel_id=1, source_target_pairs={{1,0},{2,1},{3,2},{4,3},{5,4},{6,5},{7,6},{9,8},{10,9},{11,10},{12... | collective-permute-start | bytes 589832 | tf_op jit(solution)/shard_map/while/body/eval_jaxpr/ppermute | solution.py:10
  78.5 3.2 %collective-permute-done.1 = bf16[768,128]{1,0:T(8,128)(2,1)S(1)} collective-permute-done((bf16[768,128]{1,0:T(8,128)(2,1)S(1)}, bf16[768,128]{1,0:T(8,128)(2,1)S(1)}, u32[]{:S(2)}, u32[]{:S(2)}) %collective-permute-start.1) | collective-permute-done | bytes 196640 | tf_op jit(solution)/shard_map/while/body/eval_jaxpr/ppermute | solution.py:10
  81.8 3.8 %collective-permute-start.1 = (bf16[768,128]{1,0:T(8,128)(2,1)S(1)}, bf16[768,128]{1,0:T(8,128)(2,1)S(1)}, u32[]{:S(2)}, u32[]{:S(2)}) collective-permute-start(bf16[768,128]{1,0:T(8,128)(2,1)S(1)} %copy.17), channel_id=1, source_target_pairs={{1,0},{2,1},{3,2},{4,3},{5,4},{6,5},{7,6},{9,8},{10,9},{11,10},{12... | collective-permute-start | bytes 589832 | tf_op jit(solution)/shard_map/while/body/eval_jaxpr/ppermute | solution.py:10
  85.6 3.2 %collective-permute-done.1 = bf16[768,128]{1,0:T(8,128)(2,1)S(1)} collective-permute-done((bf16[768,128]{1,0:T(8,128)(2,1)S(1)}, bf16[768,128]{1,0:T(8,128)(2,1)S(1)}, u32[]{:S(2)}, u32[]{:S(2)}) %collective-permute-start.1) | collective-permute-done | bytes 196640 | tf_op jit(solution)/shard_map/while/body/eval_jaxpr/ppermute | solution.py:10
  89.0 3.8 %collective-permute-start.1 = (bf16[768,128]{1,0:T(8,128)(2,1)S(1)}, bf16[768,128]{1,0:T(8,128)(2,1)S(1)}, u32[]{:S(2)}, u32[]{:S(2)}) collective-permute-start(bf16[768,128]{1,0:T(8,128)(2,1)S(1)} %copy.17), channel_id=1, source_target_pairs={{1,0},{2,1},{3,2},{4,3},{5,4},{6,5},{7,6},{9,8},{10,9},{11,10},{12... | collective-permute-start | bytes 589832 | tf_op jit(solution)/shard_map/while/body/eval_jaxpr/ppermute | solution.py:10
  92.8 3.2 %collective-permute-done.1 = bf16[768,128]{1,0:T(8,128)(2,1)S(1)} collective-permute-done((bf16[768,128]{1,0:T(8,128)(2,1)S(1)}, bf16[768,128]{1,0:T(8,128)(2,1)S(1)}, u32[]{:S(2)}, u32[]{:S(2)}) %collective-permute-start.1) | collective-permute-done | bytes 196640 | tf_op jit(solution)/shard_map/while/body/eval_jaxpr/ppermute | solution.py:10
  96.0 107.6 %while.37 = (s32[]{:T(128)}, bf16[768,128]{0,1:T(8,128)(2,1)S(1)}, f32[1,768]{1,0:T(1,128)S(1)}, s32[]{:T(128)}, pred[]{:T(512)}, /*index=5*/bf16[768,128]{1,0:T...) while((s32[]{:T(128)}, bf16[768,128]{0,1:T(8,128)(2,1)S(1)}, ...), condition=%wide.region_9.10_spmd.clone.clone, body=%wide.region_3.9_spmd.clone.clone.sunk | while | flops 302690304 | bytes 4156900 | solution.py:115
  96.2 1.9 collective-permute-start
  98.1 5.2 %collective-permute-done = bf16[768,128]{1,0:T(8,128)(2,1)S(1)} collective-permute-done((bf16[768,128]{1,0:T(8,128)(2,1)S(1)}, bf16[768,128]{1,0:T(8,128)(2,1)S(1)}, u32[]{:S(2)}, u32[]{:S(2)}) %collective-permute-start) | collective-permute-done | bytes 196640 | tf_op jit(solution)/shard_map/while/body/eval_jaxpr/ppermute | solution.py:10
  103.5 1.9 collective-permute-start
  105.4 5.0 %collective-permute-done = bf16[768,128]{1,0:T(8,128)(2,1)S(1)} collective-permute-done((bf16[768,128]{1,0:T(8,128)(2,1)S(1)}, bf16[768,128]{1,0:T(8,128)(2,1)S(1)}, u32[]{:S(2)}, u32[]{:S(2)}) %collective-permute-start) | collective-permute-done | bytes 196640 | tf_op jit(solution)/shard_map/while/body/eval_jaxpr/ppermute | solution.py:10
  110.7 1.9 collective-permute-start
  112.6 5.0 %collective-permute-done = bf16[768,128]{1,0:T(8,128)(2,1)S(1)} collective-permute-done((bf16[768,128]{1,0:T(8,128)(2,1)S(1)}, bf16[768,128]{1,0:T(8,128)(2,1)S(1)}, u32[]{:S(2)}, u32[]{:S(2)}) %collective-permute-start) | collective-permute-done | bytes 196640 | tf_op jit(solution)/shard_map/while/body/eval_jaxpr/ppermute | solution.py:10
  117.8 1.9 collective-permute-start
  119.8 5.0 %collective-permute-done = bf16[768,128]{1,0:T(8,128)(2,1)S(1)} collective-permute-done((bf16[768,128]{1,0:T(8,128)(2,1)S(1)}, bf16[768,128]{1,0:T(8,128)(2,1)S(1)}, u32[]{:S(2)}, u32[]{:S(2)}) %collective-permute-start) | collective-permute-done | bytes 196640 | tf_op jit(solution)/shard_map/while/body/eval_jaxpr/ppermute | solution.py:10
  125.0 1.9 collective-permute-start
  126.9 5.0 %collective-permute-done = bf16[768,128]{1,0:T(8,128)(2,1)S(1)} collective-permute-done((bf16[768,128]{1,0:T(8,128)(2,1)S(1)}, bf16[768,128]{1,0:T(8,128)(2,1)S(1)}, u32[]{:S(2)}, u32[]{:S(2)}) %collective-permute-start) | collective-permute-done | bytes 196640 | tf_op jit(solution)/shard_map/while/body/eval_jaxpr/ppermute | solution.py:10
  132.1 1.9 collective-permute-start
  134.1 5.0 %collective-permute-done = bf16[768,128]{1,0:T(8,128)(2,1)S(1)} collective-permute-done((bf16[768,128]{1,0:T(8,128)(2,1)S(1)}, bf16[768,128]{1,0:T(8,128)(2,1)S(1)}, u32[]{:S(2)}, u32[]{:S(2)}) %collective-permute-start) | collective-permute-done | bytes 196640 | tf_op jit(solution)/shard_map/while/body/eval_jaxpr/ppermute | solution.py:10
  139.3 1.9 collective-permute-start
  141.2 18.0 %collective-permute-done = bf16[768,128]{1,0:T(8,128)(2,1)S(1)} collective-permute-done((bf16[768,128]{1,0:T(8,128)(2,1)S(1)}, bf16[768,128]{1,0:T(8,128)(2,1)S(1)}, u32[]{:S(2)}, u32[]{:S(2)}) %collective-permute-start) | collective-permute-done | bytes 196640 | tf_op jit(solution)/shard_map/while/body/eval_jaxpr/ppermute | solution.py:10
  159.3 3.9 %conditional.8 = ((bf16[768,128]{0,1:T(8,128)(2,1)S(1)}, f32[1,768]{1,0:T(1,128)S(1)})) conditional(s32[]{:T(128)} %convert_element_type.148, (bf16[768,128]{0,1:T(8,128)(2,1)S(1)}, f32[1,768]{1,0:T(1,128)S(1)}) %tuple.125, (s32[4]{0:T(128)S(1)}, pred[]{:T(512)}, bf16[768,128]{1,0:T(8,128)(2,1)S(1)}, bf16[768,128]{1,0:T(8,128)(2,1)S(1)}, ...), branch_computations={%region_4.4_spmd, %region_5.8_spmd.clone} | conditional | flops 302690304 | bytes 2976905 | solution.py:84
  159.4 2.5 %multiply_reduce_fusion = (f32[768]{0:T(1024)S(1)}, bf16[768,128]{0,1:T(8,128)(2,1)S(1)}) fusion(bf16[1,768,768]{2,1,0:T(8,128)(2,1)} %get-tuple-element.827, bf16[1,768,768]{2,1,0:T(8,128)(2,1)} %get-tuple-element.826, bf16[768,128]{1,0:T(8,128)(2,1)S(1)} %get-tuple-element.824, bf16[768,128]{1,0:T(8,128)(2,1)S(1)} %get-tuple-element.825, ...), kind=kOutput, calls=%fused_computation.11 | convolution fusion | flops 302677248 | bytes 2955265 | tf_op jit(solution)/shard_map/while/body/eval_jaxpr/cond/branch_1_fun/dot_general | solution.py:52
  163.3 1.9 collective-permute-start
  165.3 5.1 %collective-permute-done = bf16[768,128]{1,0:T(8,128)(2,1)S(1)} collective-permute-done((bf16[768,128]{1,0:T(8,128)(2,1)S(1)}, bf16[768,128]{1,0:T(8,128)(2,1)S(1)}, u32[]{:S(2)}, u32[]{:S(2)}) %collective-permute-start) | collective-permute-done | bytes 196640 | tf_op jit(solution)/shard_map/while/body/eval_jaxpr/ppermute | solution.py:10
  170.3 3.9 %conditional.8 = ((bf16[768,128]{0,1:T(8,128)(2,1)S(1)}, f32[1,768]{1,0:T(1,128)S(1)})) conditional(s32[]{:T(128)} %convert_element_type.148, (bf16[768,128]{0,1:T(8,128)(2,1)S(1)}, f32[1,768]{1,0:T(1,128)S(1)}) %tuple.125, (s32[4]{0:T(128)S(1)}, pred[]{:T(512)}, bf16[768,128]{1,0:T(8,128)(2,1)S(1)}, bf16[768,128]{1,0:T(8,128)(2,1)S(1)}, ...), branch_computations={%region_4.4_spmd, %region_5.8_spmd.clone} | conditional | flops 302690304 | bytes 2976905 | solution.py:84
  170.4 2.5 %multiply_reduce_fusion = (f32[768]{0:T(1024)S(1)}, bf16[768,128]{0,1:T(8,128)(2,1)S(1)}) fusion(bf16[1,768,768]{2,1,0:T(8,128)(2,1)} %get-tuple-element.827, bf16[1,768,768]{2,1,0:T(8,128)(2,1)} %get-tuple-element.826, bf16[768,128]{1,0:T(8,128)(2,1)S(1)} %get-tuple-element.824, bf16[768,128]{1,0:T(8,128)(2,1)S(1)} %get-tuple-element.825, ...), kind=kOutput, calls=%fused_computation.11 | convolution fusion | flops 302677248 | bytes 2955265 | tf_op jit(solution)/shard_map/while/body/eval_jaxpr/cond/branch_1_fun/dot_general | solution.py:52
  174.4 1.9 collective-permute-start
  176.4 5.0 %collective-permute-done = bf16[768,128]{1,0:T(8,128)(2,1)S(1)} collective-permute-done((bf16[768,128]{1,0:T(8,128)(2,1)S(1)}, bf16[768,128]{1,0:T(8,128)(2,1)S(1)}, u32[]{:S(2)}, u32[]{:S(2)}) %collective-permute-start) | collective-permute-done | bytes 196640 | tf_op jit(solution)/shard_map/while/body/eval_jaxpr/ppermute | solution.py:10
  181.4 3.9 %conditional.8 = ((bf16[768,128]{0,1:T(8,128)(2,1)S(1)}, f32[1,768]{1,0:T(1,128)S(1)})) conditional(s32[]{:T(128)} %convert_element_type.148, (bf16[768,128]{0,1:T(8,128)(2,1)S(1)}, f32[1,768]{1,0:T(1,128)S(1)}) %tuple.125, (s32[4]{0:T(128)S(1)}, pred[]{:T(512)}, bf16[768,128]{1,0:T(8,128)(2,1)S(1)}, bf16[768,128]{1,0:T(8,128)(2,1)S(1)}, ...), branch_computations={%region_4.4_spmd, %region_5.8_spmd.clone} | conditional | flops 302690304 | bytes 2976905 | solution.py:84
  181.5 2.5 %multiply_reduce_fusion = (f32[768]{0:T(1024)S(1)}, bf16[768,128]{0,1:T(8,128)(2,1)S(1)}) fusion(bf16[1,768,768]{2,1,0:T(8,128)(2,1)} %get-tuple-element.827, bf16[1,768,768]{2,1,0:T(8,128)(2,1)} %get-tuple-element.826, bf16[768,128]{1,0:T(8,128)(2,1)S(1)} %get-tuple-element.824, bf16[768,128]{1,0:T(8,128)(2,1)S(1)} %get-tuple-element.825, ...), kind=kOutput, calls=%fused_computation.11 | convolution fusion | flops 302677248 | bytes 2955265 | tf_op jit(solution)/shard_map/while/body/eval_jaxpr/cond/branch_1_fun/dot_general | solution.py:52
  185.5 1.9 collective-permute-start
  187.4 5.0 %collective-permute-done = bf16[768,128]{1,0:T(8,128)(2,1)S(1)} collective-permute-done((bf16[768,128]{1,0:T(8,128)(2,1)S(1)}, bf16[768,128]{1,0:T(8,128)(2,1)S(1)}, u32[]{:S(2)}, u32[]{:S(2)}) %collective-permute-start) | collective-permute-done | bytes 196640 | tf_op jit(solution)/shard_map/while/body/eval_jaxpr/ppermute | solution.py:10
  192.5 3.9 %conditional.8 = ((bf16[768,128]{0,1:T(8,128)(2,1)S(1)}, f32[1,768]{1,0:T(1,128)S(1)})) conditional(s32[]{:T(128)} %convert_element_type.148, (bf16[768,128]{0,1:T(8,128)(2,1)S(1)}, f32[1,768]{1,0:T(1,128)S(1)}) %tuple.125, (s32[4]{0:T(128)S(1)}, pred[]{:T(512)}, bf16[768,128]{1,0:T(8,128)(2,1)S(1)}, bf16[768,128]{1,0:T(8,128)(2,1)S(1)}, ...), branch_computations={%region_4.4_spmd, %region_5.8_spmd.clone} | conditional | flops 302690304 | bytes 2976905 | solution.py:84
  192.6 2.5 %multiply_reduce_fusion = (f32[768]{0:T(1024)S(1)}, bf16[768,128]{0,1:T(8,128)(2,1)S(1)}) fusion(bf16[1,768,768]{2,1,0:T(8,128)(2,1)} %get-tuple-element.827, bf16[1,768,768]{2,1,0:T(8,128)(2,1)} %get-tuple-element.826, bf16[768,128]{1,0:T(8,128)(2,1)S(1)} %get-tuple-element.824, bf16[768,128]{1,0:T(8,128)(2,1)S(1)} %get-tuple-element.825, ...), kind=kOutput, calls=%fused_computation.11 | convolution fusion | flops 302677248 | bytes 2955265 | tf_op jit(solution)/shard_map/while/body/eval_jaxpr/cond/branch_1_fun/dot_general | solution.py:52
  196.6 1.9 collective-permute-start
  198.5 5.0 %collective-permute-done = bf16[768,128]{1,0:T(8,128)(2,1)S(1)} collective-permute-done((bf16[768,128]{1,0:T(8,128)(2,1)S(1)}, bf16[768,128]{1,0:T(8,128)(2,1)S(1)}, u32[]{:S(2)}, u32[]{:S(2)}) %collective-permute-start) | collective-permute-done | bytes 196640 | tf_op jit(solution)/shard_map/while/body/eval_jaxpr/ppermute | solution.py:10
  203.6 10.5 %psum.7 = f32[1,768]{1,0:T(1,128)} all-reduce(f32[1,768]{1,0:T(1,128)S(1)} %add.52), channel_id=1, replica_groups=mesh['energy'=4,'slab'=8] {'energy'}, use_global_device_ids=true, to_apply=%region_17.18 | all-reduce | flops 768 | bytes 6144 | tf_op jit(solution)/shard_map/psum | solution.py:117
  (108 shorter events, 15.2 us)
Async XLA Ops:
  2.4 93.6 %copy-start = (bf16[768,128]{1,0:T(8,128)(2,1)S(1)}, bf16[768,128]{1,0:T(8,128)(2,1)}, u32[]{:S(2)}) copy-start(bf16[768,128]{1,0:T(8,128)(2,1)} %param.24) | copy-start | bytes 589828
  2.6 5.1 %collective-permute-start.1 = (bf16[768,128]{1,0:T(8,128)(2,1)S(1)}, bf16[768,128]{1,0:T(8,128)(2,1)S(1)}, u32[]{:S(2)}, u32[]{:S(2)}) collective-permute-start(bf16[768,128]{1,0:T(8,128)(2,1)S(1)} %copy.17), channel_id=1, source_target_pairs={{1,0},{2,1},{3,2},{4,3},{5,4},{6,5},{7,6},{9,8},{10,9},{11,10},{12... | collective-permute-start | bytes 589832 | tf_op jit(solution)/shard_map/while/body/eval_jaxpr/ppermute | solution.py:10
  7.9 7.0 %collective-permute-start.1 = (bf16[768,128]{1,0:T(8,128)(2,1)S(1)}, bf16[768,128]{1,0:T(8,128)(2,1)S(1)}, u32[]{:S(2)}, u32[]{:S(2)}) collective-permute-start(bf16[768,128]{1,0:T(8,128)(2,1)S(1)} %copy.17), channel_id=1, source_target_pairs={{1,0},{2,1},{3,2},{4,3},{5,4},{6,5},{7,6},{9,8},{10,9},{11,10},{12... | collective-permute-start | bytes 589832 | tf_op jit(solution)/shard_map/while/body/eval_jaxpr/ppermute | solution.py:10
  18.8 5.1 %collective-permute-start.1 = (bf16[768,128]{1,0:T(8,128)(2,1)S(1)}, bf16[768,128]{1,0:T(8,128)(2,1)S(1)}, u32[]{:S(2)}, u32[]{:S(2)}) collective-permute-start(bf16[768,128]{1,0:T(8,128)(2,1)S(1)} %copy.17), channel_id=1, source_target_pairs={{1,0},{2,1},{3,2},{4,3},{5,4},{6,5},{7,6},{9,8},{10,9},{11,10},{12... | collective-permute-start | bytes 589832 | tf_op jit(solution)/shard_map/while/body/eval_jaxpr/ppermute | solution.py:10
  27.7 7.0 %collective-permute-start.1 = (bf16[768,128]{1,0:T(8,128)(2,1)S(1)}, bf16[768,128]{1,0:T(8,128)(2,1)S(1)}, u32[]{:S(2)}, u32[]{:S(2)}) collective-permute-start(bf16[768,128]{1,0:T(8,128)(2,1)S(1)} %copy.17), channel_id=1, source_target_pairs={{1,0},{2,1},{3,2},{4,3},{5,4},{6,5},{7,6},{9,8},{10,9},{11,10},{12... | collective-permute-start | bytes 589832 | tf_op jit(solution)/shard_map/while/body/eval_jaxpr/ppermute | solution.py:10
  38.6 7.0 %collective-permute-start.1 = (bf16[768,128]{1,0:T(8,128)(2,1)S(1)}, bf16[768,128]{1,0:T(8,128)(2,1)S(1)}, u32[]{:S(2)}, u32[]{:S(2)}) collective-permute-start(bf16[768,128]{1,0:T(8,128)(2,1)S(1)} %copy.17), channel_id=1, source_target_pairs={{1,0},{2,1},{3,2},{4,3},{5,4},{6,5},{7,6},{9,8},{10,9},{11,10},{12... | collective-permute-start | bytes 589832 | tf_op jit(solution)/shard_map/while/body/eval_jaxpr/ppermute | solution.py:10
  49.5 7.0 %collective-permute-start.1 = (bf16[768,128]{1,0:T(8,128)(2,1)S(1)}, bf16[768,128]{1,0:T(8,128)(2,1)S(1)}, u32[]{:S(2)}, u32[]{:S(2)}) collective-permute-start(bf16[768,128]{1,0:T(8,128)(2,1)S(1)} %copy.17), channel_id=1, source_target_pairs={{1,0},{2,1},{3,2},{4,3},{5,4},{6,5},{7,6},{9,8},{10,9},{11,10},{12... | collective-permute-start | bytes 589832 | tf_op jit(solution)/shard_map/while/body/eval_jaxpr/ppermute | solution.py:10
  56.6 10.7 %collective-permute-start.1 = (bf16[768,128]{1,0:T(8,128)(2,1)S(1)}, bf16[768,128]{1,0:T(8,128)(2,1)S(1)}, u32[]{:S(2)}, u32[]{:S(2)}) collective-permute-start(bf16[768,128]{1,0:T(8,128)(2,1)S(1)} %copy.17), channel_id=1, source_target_pairs={{1,0},{2,1},{3,2},{4,3},{5,4},{6,5},{7,6},{9,8},{10,9},{11,10},{12... | collective-permute-start | bytes 589832 | tf_op jit(solution)/shard_map/while/body/eval_jaxpr/ppermute | solution.py:10
  67.5 7.0 %collective-permute-start.1 = (bf16[768,128]{1,0:T(8,128)(2,1)S(1)}, bf16[768,128]{1,0:T(8,128)(2,1)S(1)}, u32[]{:S(2)}, u32[]{:S(2)}) collective-permute-start(bf16[768,128]{1,0:T(8,128)(2,1)S(1)} %copy.17), channel_id=1, source_target_pairs={{1,0},{2,1},{3,2},{4,3},{5,4},{6,5},{7,6},{9,8},{10,9},{11,10},{12... | collective-permute-start | bytes 589832 | tf_op jit(solution)/shard_map/while/body/eval_jaxpr/ppermute | solution.py:10
  74.7 7.0 %collective-permute-start.1 = (bf16[768,128]{1,0:T(8,128)(2,1)S(1)}, bf16[768,128]{1,0:T(8,128)(2,1)S(1)}, u32[]{:S(2)}, u32[]{:S(2)}) collective-permute-start(bf16[768,128]{1,0:T(8,128)(2,1)S(1)} %copy.17), channel_id=1, source_target_pairs={{1,0},{2,1},{3,2},{4,3},{5,4},{6,5},{7,6},{9,8},{10,9},{11,10},{12... | collective-permute-start | bytes 589832 | tf_op jit(solution)/shard_map/while/body/eval_jaxpr/ppermute | solution.py:10
  81.8 7.0 %collective-permute-start.1 = (bf16[768,128]{1,0:T(8,128)(2,1)S(1)}, bf16[768,128]{1,0:T(8,128)(2,1)S(1)}, u32[]{:S(2)}, u32[]{:S(2)}) collective-permute-start(bf16[768,128]{1,0:T(8,128)(2,1)S(1)} %copy.17), channel_id=1, source_target_pairs={{1,0},{2,1},{3,2},{4,3},{5,4},{6,5},{7,6},{9,8},{10,9},{11,10},{12... | collective-permute-start | bytes 589832 | tf_op jit(solution)/shard_map/while/body/eval_jaxpr/ppermute | solution.py:10
  89.0 7.0 %collective-permute-start.1 = (bf16[768,128]{1,0:T(8,128)(2,1)S(1)}, bf16[768,128]{1,0:T(8,128)(2,1)S(1)}, u32[]{:S(2)}, u32[]{:S(2)}) collective-permute-start(bf16[768,128]{1,0:T(8,128)(2,1)S(1)} %copy.17), channel_id=1, source_target_pairs={{1,0},{2,1},{3,2},{4,3},{5,4},{6,5},{7,6},{9,8},{10,9},{11,10},{12... | collective-permute-start | bytes 589832 | tf_op jit(solution)/shard_map/while/body/eval_jaxpr/ppermute | solution.py:10
  96.2 7.2 %collective-permute-start = (bf16[768,128]{1,0:T(8,128)(2,1)S(1)}, bf16[768,128]{1,0:T(8,128)(2,1)S(1)}, u32[]{:S(2)}, u32[]{:S(2)}) collective-permute-start(bf16[768,128]{1,0:T(8,128)(2,1)S(1)} %copy.16), channel_id=1, source_target_pairs={{0,1},{1,2},{2,3},{3,4},{4,5},{5,6},{6,7},{8,9},{9,10},{10,11},{11... | collective-permute-start | bytes 589832 | tf_op jit(solution)/shard_map/while/body/eval_jaxpr/ppermute | solution.py:10
  103.5 7.0 %collective-permute-start = (bf16[768,128]{1,0:T(8,128)(2,1)S(1)}, bf16[768,128]{1,0:T(8,128)(2,1)S(1)}, u32[]{:S(2)}, u32[]{:S(2)}) collective-permute-start(bf16[768,128]{1,0:T(8,128)(2,1)S(1)} %copy.16), channel_id=1, source_target_pairs={{0,1},{1,2},{2,3},{3,4},{4,5},{5,6},{6,7},{8,9},{9,10},{10,11},{11... | collective-permute-start | bytes 589832 | tf_op jit(solution)/shard_map/while/body/eval_jaxpr/ppermute | solution.py:10
  110.7 7.0 %collective-permute-start = (bf16[768,128]{1,0:T(8,128)(2,1)S(1)}, bf16[768,128]{1,0:T(8,128)(2,1)S(1)}, u32[]{:S(2)}, u32[]{:S(2)}) collective-permute-start(bf16[768,128]{1,0:T(8,128)(2,1)S(1)} %copy.16), channel_id=1, source_target_pairs={{0,1},{1,2},{2,3},{3,4},{4,5},{5,6},{6,7},{8,9},{9,10},{10,11},{11... | collective-permute-start | bytes 589832 | tf_op jit(solution)/shard_map/while/body/eval_jaxpr/ppermute | solution.py:10
  117.8 7.0 %collective-permute-start = (bf16[768,128]{1,0:T(8,128)(2,1)S(1)}, bf16[768,128]{1,0:T(8,128)(2,1)S(1)}, u32[]{:S(2)}, u32[]{:S(2)}) collective-permute-start(bf16[768,128]{1,0:T(8,128)(2,1)S(1)} %copy.16), channel_id=1, source_target_pairs={{0,1},{1,2},{2,3},{3,4},{4,5},{5,6},{6,7},{8,9},{9,10},{10,11},{11... | collective-permute-start | bytes 589832 | tf_op jit(solution)/shard_map/while/body/eval_jaxpr/ppermute | solution.py:10
  125.0 7.0 %collective-permute-start = (bf16[768,128]{1,0:T(8,128)(2,1)S(1)}, bf16[768,128]{1,0:T(8,128)(2,1)S(1)}, u32[]{:S(2)}, u32[]{:S(2)}) collective-permute-start(bf16[768,128]{1,0:T(8,128)(2,1)S(1)} %copy.16), channel_id=1, source_target_pairs={{0,1},{1,2},{2,3},{3,4},{4,5},{5,6},{6,7},{8,9},{9,10},{10,11},{11... | collective-permute-start | bytes 589832 | tf_op jit(solution)/shard_map/while/body/eval_jaxpr/ppermute | solution.py:10
  132.1 7.0 %collective-permute-start = (bf16[768,128]{1,0:T(8,128)(2,1)S(1)}, bf16[768,128]{1,0:T(8,128)(2,1)S(1)}, u32[]{:S(2)}, u32[]{:S(2)}) collective-permute-start(bf16[768,128]{1,0:T(8,128)(2,1)S(1)} %copy.16), channel_id=1, source_target_pairs={{0,1},{1,2},{2,3},{3,4},{4,5},{5,6},{6,7},{8,9},{9,10},{10,11},{11... | collective-permute-start | bytes 589832 | tf_op jit(solution)/shard_map/while/body/eval_jaxpr/ppermute | solution.py:10
  139.3 20.0 %collective-permute-start = (bf16[768,128]{1,0:T(8,128)(2,1)S(1)}, bf16[768,128]{1,0:T(8,128)(2,1)S(1)}, u32[]{:S(2)}, u32[]{:S(2)}) collective-permute-start(bf16[768,128]{1,0:T(8,128)(2,1)S(1)} %copy.16), channel_id=1, source_target_pairs={{0,1},{1,2},{2,3},{3,4},{4,5},{5,6},{6,7},{8,9},{9,10},{10,11},{11... | collective-permute-start | bytes 589832 | tf_op jit(solution)/shard_map/while/body/eval_jaxpr/ppermute | solution.py:10
  163.3 7.0 %collective-permute-start = (bf16[768,128]{1,0:T(8,128)(2,1)S(1)}, bf16[768,128]{1,0:T(8,128)(2,1)S(1)}, u32[]{:S(2)}, u32[]{:S(2)}) collective-permute-start(bf16[768,128]{1,0:T(8,128)(2,1)S(1)} %copy.16), channel_id=1, source_target_pairs={{0,1},{1,2},{2,3},{3,4},{4,5},{5,6},{6,7},{8,9},{9,10},{10,11},{11... | collective-permute-start | bytes 589832 | tf_op jit(solution)/shard_map/while/body/eval_jaxpr/ppermute | solution.py:10
  174.4 7.0 %collective-permute-start = (bf16[768,128]{1,0:T(8,128)(2,1)S(1)}, bf16[768,128]{1,0:T(8,128)(2,1)S(1)}, u32[]{:S(2)}, u32[]{:S(2)}) collective-permute-start(bf16[768,128]{1,0:T(8,128)(2,1)S(1)} %copy.16), channel_id=1, source_target_pairs={{0,1},{1,2},{2,3},{3,4},{4,5},{5,6},{6,7},{8,9},{9,10},{10,11},{11... | collective-permute-start | bytes 589832 | tf_op jit(solution)/shard_map/while/body/eval_jaxpr/ppermute | solution.py:10
  185.5 7.0 %collective-permute-start = (bf16[768,128]{1,0:T(8,128)(2,1)S(1)}, bf16[768,128]{1,0:T(8,128)(2,1)S(1)}, u32[]{:S(2)}, u32[]{:S(2)}) collective-permute-start(bf16[768,128]{1,0:T(8,128)(2,1)S(1)} %copy.16), channel_id=1, source_target_pairs={{0,1},{1,2},{2,3},{3,4},{4,5},{5,6},{6,7},{8,9},{9,10},{10,11},{11... | collective-permute-start | bytes 589832 | tf_op jit(solution)/shard_map/while/body/eval_jaxpr/ppermute | solution.py:10
  196.6 7.0 %collective-permute-start = (bf16[768,128]{1,0:T(8,128)(2,1)S(1)}, bf16[768,128]{1,0:T(8,128)(2,1)S(1)}, u32[]{:S(2)}, u32[]{:S(2)}) collective-permute-start(bf16[768,128]{1,0:T(8,128)(2,1)S(1)} %copy.16), channel_id=1, source_target_pairs={{0,1},{1,2},{2,3},{3,4},{4,5},{5,6},{6,7},{8,9},{9,10},{10,11},{11... | collective-permute-start | bytes 589832 | tf_op jit(solution)/shard_map/while/body/eval_jaxpr/ppermute | solution.py:10
where the time goes:
time: 215 us; the launch traced here: 214 us
  waiting for transfers between devices  103 us (48%)
  starting transfers between devices  63 us (29%)
  matrix products  19.5 us (9%)
  other arithmetic  12.4 us (6%)
  blocking collectives  10.5 us (5%)
  local copies, waits for them, and re-layouts  3.61 us (2%)
    ppermute x22, waiting for transfers between devices, passed_along(): return lax.ppermute(block, axis, route)  103 us
    ppermute x22, starting transfers between devices, passed_along(): return lax.ppermute(block, axis, route)  63 us
    psum x1, blocking collectives, local(): return lax.psum(forward_density + backward_density, 'energy')  10.5 us
    dot_general x4, matrix products, sweep_down(): jnp.dot(left_basis[0], scaled, preferred_element_type=jnp.float32)  10.1 us
    dot_general x4, matrix products, sweep_up(): jnp.einsum('wv,wm->vm', right_basis[index], scaled, preferred_element_typ...  9.33 us
    reduce_sum x8, other arithmetic, select(): jnp.sum(chosen * weight)  4.96 us
    mul x8, other arithmetic, contribution(): return scale * jnp.sum(squared, axis=1)  4.91 us
  transfers between devices with their start and end apart: 22, of which 22 were waited for; matrix products, arithmetic and copies ran while one was open for 0% of the time, Pallas kernels for 0%

commit v1 on v0

--- a/solution.py
+++ b/solution.py
@@ -114,7 +114,8 @@
 
     _, forward_density = lax.fori_loop(0, turns, forward_turn, (zero_state, zero_density))
     _, backward_density = lax.fori_loop(0, turns, backward_turn, (zero_state, zero_density))
-    return lax.psum(forward_density + backward_density, "energy")
+    clear_local_data_on_mesh = lambda xs: lax.all_gather(xs, axis_name="energy").sum(axis=0)
+    return clear_local_data_on_mesh(forward_density + backward_density)
 
 
 def solution(mesh):

time: 215 us -> 213 us (level)
  blocking collectives: 10.5 us -> 8.16 us
    psum x1 -> x0, blocking collectives: 10.5 us -> none  [local(): return lax.psum(forward_density + backward_density, 'energy')]
    all_gather x0 -> x1, blocking collectives: none -> 8.16 us  [local(): lax.all_gather(xs, axis_name='energy').sum(axis=0)]
where the time goes in v1:
time: 213 us; the launch traced here: 212 us
  waiting for transfers between devices  103 us (48%)
  starting transfers between devices  63 us (30%)
  matrix products  19.5 us (9%)
  other arithmetic  12.5 us (6%)
  blocking collectives  8.16 us (4%)
  local copies, waits for them, and re-layouts  4.19 us (2%)
    ppermute x22, waiting for transfers between devices, passed_along(): return lax.ppermute(block, axis, route)  103 us
    ppermute x22, starting transfers between devices, passed_along(): return lax.ppermute(block, axis, route)  63 us
    dot_general x4, matrix products, sweep_down(): jnp.dot(left_basis[0], scaled, preferred_element_type=jnp.float32)  10.1 us
    dot_general x4, matrix products, sweep_up(): jnp.einsum('wv,wm->vm', right_basis[index], scaled, preferred_element_typ...  9.33 us
    all_gather x1, blocking collectives, local(): lax.all_gather(xs, axis_name='energy').sum(axis=0)  8.16 us
    reduce_sum x8, other arithmetic, select(): jnp.sum(chosen * weight)  4.96 us
    mul x8, other arithmetic, contribution(): return scale * jnp.sum(squared, axis=1)  4.91 us
  transfers between devices with their start and end apart: 22, of which 22 were waited for; matrix products, arithmetic and copies ran while one was open for 0% of the time, Pallas kernels for 0%

profile of v1, /device:TPU:24, one launch (start us, length us, event | category | flops | bytes accessed | tf_op | source)
XLA Modules:
  0.0 212.3 jit_solution(15903932243232067528)
XLA Ops:
  0.0 0.9 select_reduce_fusion.1
  2.4 93.5 %while.38 = (s32[]{:T(128)}, bf16[768,128]{0,1:T(8,128)(2,1)S(1)}, f32[1,768]{1,0:T(1,128)S(1)}, s32[]{:T(128)}, pred[]{:T(512)}, /*index=5*/bf16[768,128]{1,0:T...) while((s32[]{:T(128)}, bf16[768,128]{0,1:T(8,128)(2,1)S(1)}, ...), condition=%wide.region_16.17_spmd.clone.clone, body=%wide.region_10.16_spmd.clone.clone.sunk | while | flops 302690304 | bytes 4156900 | solution.py:116
  2.6 1.9 collective-permute-start.1
  4.6 3.2 %collective-permute-done.1 = bf16[768,128]{1,0:T(8,128)(2,1)S(1)} collective-permute-done((bf16[768,128]{1,0:T(8,128)(2,1)S(1)}, bf16[768,128]{1,0:T(8,128)(2,1)S(1)}, u32[]{:S(2)}, u32[]{:S(2)}) %collective-permute-start.1) | collective-permute-done | bytes 196640 | tf_op jit(solution)/shard_map/while/body/eval_jaxpr/ppermute | solution.py:10
  7.9 3.8 %collective-permute-start.1 = (bf16[768,128]{1,0:T(8,128)(2,1)S(1)}, bf16[768,128]{1,0:T(8,128)(2,1)S(1)}, u32[]{:S(2)}, u32[]{:S(2)}) collective-permute-start(bf16[768,128]{1,0:T(8,128)(2,1)S(1)} %copy.19), channel_id=1, source_target_pairs={{1,0},{2,1},{3,2},{4,3},{5,4},{6,5},{7,6},{9,8},{10,9},{11,10},{12... | collective-permute-start | bytes 589832 | tf_op jit(solution)/shard_map/while/body/eval_jaxpr/ppermute | solution.py:10
  11.7 3.2 %collective-permute-done.1 = bf16[768,128]{1,0:T(8,128)(2,1)S(1)} collective-permute-done((bf16[768,128]{1,0:T(8,128)(2,1)S(1)}, bf16[768,128]{1,0:T(8,128)(2,1)S(1)}, u32[]{:S(2)}, u32[]{:S(2)}) %collective-permute-start.1) | collective-permute-done | bytes 196640 | tf_op jit(solution)/shard_map/while/body/eval_jaxpr/ppermute | solution.py:10
  14.9 3.7 %conditional.9 = ((bf16[768,128]{0,1:T(8,128)(2,1)S(1)}, f32[1,768]{1,0:T(1,128)S(1)})) conditional(s32[]{:T(128)} %convert_element_type.149, (bf16[768,128]{0,1:T(8,128)(2,1)S(1)}, f32[1,768]{1,0:T(1,128)S(1)}) %tuple.128, (s32[4]{0:T(128)S(1)}, pred[]{:T(512)}, bf16[768,128]{1,0:T(8,128)(2,1)}, bf16[768,128]{1,0:T(8,128)(2,1)S(1)}, ...), branch_computations={%region_11.11_spmd, %region_12.15_spmd.clone} | conditional | flops 302690304 | bytes 2976905 | solution.py:99
  15.0 2.3 %multiply_reduce_fusion.1 = (f32[768]{0:T(1024)S(1)}, bf16[768,128]{0,1:T(8,128)(2,1)S(1)}) fusion(bf16[1,768,768]{2,1,0:T(8,128)(2,1)} %get-tuple-element.853, bf16[1,768,768]{2,1,0:T(8,128)(2,1)} %get-tuple-element.852, bf16[768,128]{1,0:T(8,128)(2,1)} %get-tuple-element.850, bf16[768,128]{1,0:T(8,128)(2,1)S(1)} %get-tuple-element.851, ...), kind=kOutput, calls=%fused_computation.30 | convolution fusion | flops 302677248 | bytes 2955265 | tf_op jit(solution)/shard_map/while/body/eval_jaxpr/cond/branch_1_fun/wv,wm->vm/dot_general | solution.py:65
  18.8 1.9 collective-permute-start.1
  20.7 3.2 %collective-permute-done.1 = bf16[768,128]{1,0:T(8,128)(2,1)S(1)} collective-permute-done((bf16[768,128]{1,0:T(8,128)(2,1)S(1)}, bf16[768,128]{1,0:T(8,128)(2,1)S(1)}, u32[]{:S(2)}, u32[]{:S(2)}) %collective-permute-start.1) | collective-permute-done | bytes 196640 | tf_op jit(solution)/shard_map/while/body/eval_jaxpr/ppermute | solution.py:10
  23.9 3.7 %conditional.9 = ((bf16[768,128]{0,1:T(8,128)(2,1)S(1)}, f32[1,768]{1,0:T(1,128)S(1)})) conditional(s32[]{:T(128)} %convert_element_type.149, (bf16[768,128]{0,1:T(8,128)(2,1)S(1)}, f32[1,768]{1,0:T(1,128)S(1)}) %tuple.128, (s32[4]{0:T(128)S(1)}, pred[]{:T(512)}, bf16[768,128]{1,0:T(8,128)(2,1)}, bf16[768,128]{1,0:T(8,128)(2,1)S(1)}, ...), branch_computations={%region_11.11_spmd, %region_12.15_spmd.clone} | conditional | flops 302690304 | bytes 2976905 | solution.py:99
  24.0 2.3 %multiply_reduce_fusion.1 = (f32[768]{0:T(1024)S(1)}, bf16[768,128]{0,1:T(8,128)(2,1)S(1)}) fusion(bf16[1,768,768]{2,1,0:T(8,128)(2,1)} %get-tuple-element.853, bf16[1,768,768]{2,1,0:T(8,128)(2,1)} %get-tuple-element.852, bf16[768,128]{1,0:T(8,128)(2,1)} %get-tuple-element.850, bf16[768,128]{1,0:T(8,128)(2,1)S(1)} %get-tuple-element.851, ...), kind=kOutput, calls=%fused_computation.30 | convolution fusion | flops 302677248 | bytes 2955265 | tf_op jit(solution)/shard_map/while/body/eval_jaxpr/cond/branch_1_fun/wv,wm->vm/dot_general | solution.py:65
  27.7 3.8 %collective-permute-start.1 = (bf16[768,128]{1,0:T(8,128)(2,1)S(1)}, bf16[768,128]{1,0:T(8,128)(2,1)S(1)}, u32[]{:S(2)}, u32[]{:S(2)}) collective-permute-start(bf16[768,128]{1,0:T(8,128)(2,1)S(1)} %copy.19), channel_id=1, source_target_pairs={{1,0},{2,1},{3,2},{4,3},{5,4},{6,5},{7,6},{9,8},{10,9},{11,10},{12... | collective-permute-start | bytes 589832 | tf_op jit(solution)/shard_map/while/body/eval_jaxpr/ppermute | solution.py:10
  31.6 3.2 %collective-permute-done.1 = bf16[768,128]{1,0:T(8,128)(2,1)S(1)} collective-permute-done((bf16[768,128]{1,0:T(8,128)(2,1)S(1)}, bf16[768,128]{1,0:T(8,128)(2,1)S(1)}, u32[]{:S(2)}, u32[]{:S(2)}) %collective-permute-start.1) | collective-permute-done | bytes 196640 | tf_op jit(solution)/shard_map/while/body/eval_jaxpr/ppermute | solution.py:10
  34.7 3.7 %conditional.9 = ((bf16[768,128]{0,1:T(8,128)(2,1)S(1)}, f32[1,768]{1,0:T(1,128)S(1)})) conditional(s32[]{:T(128)} %convert_element_type.149, (bf16[768,128]{0,1:T(8,128)(2,1)S(1)}, f32[1,768]{1,0:T(1,128)S(1)}) %tuple.128, (s32[4]{0:T(128)S(1)}, pred[]{:T(512)}, bf16[768,128]{1,0:T(8,128)(2,1)}, bf16[768,128]{1,0:T(8,128)(2,1)S(1)}, ...), branch_computations={%region_11.11_spmd, %region_12.15_spmd.clone} | conditional | flops 302690304 | bytes 2976905 | solution.py:99
  34.8 2.3 %multiply_reduce_fusion.1 = (f32[768]{0:T(1024)S(1)}, bf16[768,128]{0,1:T(8,128)(2,1)S(1)}) fusion(bf16[1,768,768]{2,1,0:T(8,128)(2,1)} %get-tuple-element.853, bf16[1,768,768]{2,1,0:T(8,128)(2,1)} %get-tuple-element.852, bf16[768,128]{1,0:T(8,128)(2,1)} %get-tuple-element.850, bf16[768,128]{1,0:T(8,128)(2,1)S(1)} %get-tuple-element.851, ...), kind=kOutput, calls=%fused_computation.30 | convolution fusion | flops 302677248 | bytes 2955265 | tf_op jit(solution)/shard_map/while/body/eval_jaxpr/cond/branch_1_fun/wv,wm->vm/dot_general | solution.py:65
  38.6 3.8 %collective-permute-start.1 = (bf16[768,128]{1,0:T(8,128)(2,1)S(1)}, bf16[768,128]{1,0:T(8,128)(2,1)S(1)}, u32[]{:S(2)}, u32[]{:S(2)}) collective-permute-start(bf16[768,128]{1,0:T(8,128)(2,1)S(1)} %copy.19), channel_id=1, source_target_pairs={{1,0},{2,1},{3,2},{4,3},{5,4},{6,5},{7,6},{9,8},{10,9},{11,10},{12... | collective-permute-start | bytes 589832 | tf_op jit(solution)/shard_map/while/body/eval_jaxpr/ppermute | solution.py:10
  42.4 3.2 %collective-permute-done.1 = bf16[768,128]{1,0:T(8,128)(2,1)S(1)} collective-permute-done((bf16[768,128]{1,0:T(8,128)(2,1)S(1)}, bf16[768,128]{1,0:T(8,128)(2,1)S(1)}, u32[]{:S(2)}, u32[]{:S(2)}) %collective-permute-start.1) | collective-permute-done | bytes 196640 | tf_op jit(solution)/shard_map/while/body/eval_jaxpr/ppermute | solution.py:10
  45.6 3.7 %conditional.9 = ((bf16[768,128]{0,1:T(8,128)(2,1)S(1)}, f32[1,768]{1,0:T(1,128)S(1)})) conditional(s32[]{:T(128)} %convert_element_type.149, (bf16[768,128]{0,1:T(8,128)(2,1)S(1)}, f32[1,768]{1,0:T(1,128)S(1)}) %tuple.128, (s32[4]{0:T(128)S(1)}, pred[]{:T(512)}, bf16[768,128]{1,0:T(8,128)(2,1)}, bf16[768,128]{1,0:T(8,128)(2,1)S(1)}, ...), branch_computations={%region_11.11_spmd, %region_12.15_spmd.clone} | conditional | flops 302690304 | bytes 2976905 | solution.py:99
  45.7 2.3 %multiply_reduce_fusion.1 = (f32[768]{0:T(1024)S(1)}, bf16[768,128]{0,1:T(8,128)(2,1)S(1)}) fusion(bf16[1,768,768]{2,1,0:T(8,128)(2,1)} %get-tuple-element.853, bf16[1,768,768]{2,1,0:T(8,128)(2,1)} %get-tuple-element.852, bf16[768,128]{1,0:T(8,128)(2,1)} %get-tuple-element.850, bf16[768,128]{1,0:T(8,128)(2,1)S(1)} %get-tuple-element.851, ...), kind=kOutput, calls=%fused_computation.30 | convolution fusion | flops 302677248 | bytes 2955265 | tf_op jit(solution)/shard_map/while/body/eval_jaxpr/cond/branch_1_fun/wv,wm->vm/dot_general | solution.py:65
  49.5 3.8 %collective-permute-start.1 = (bf16[768,128]{1,0:T(8,128)(2,1)S(1)}, bf16[768,128]{1,0:T(8,128)(2,1)S(1)}, u32[]{:S(2)}, u32[]{:S(2)}) collective-permute-start(bf16[768,128]{1,0:T(8,128)(2,1)S(1)} %copy.19), channel_id=1, source_target_pairs={{1,0},{2,1},{3,2},{4,3},{5,4},{6,5},{7,6},{9,8},{10,9},{11,10},{12... | collective-permute-start | bytes 589832 | tf_op jit(solution)/shard_map/while/body/eval_jaxpr/ppermute | solution.py:10
  53.3 3.2 %collective-permute-done.1 = bf16[768,128]{1,0:T(8,128)(2,1)S(1)} collective-permute-done((bf16[768,128]{1,0:T(8,128)(2,1)S(1)}, bf16[768,128]{1,0:T(8,128)(2,1)S(1)}, u32[]{:S(2)}, u32[]{:S(2)}) %collective-permute-start.1) | collective-permute-done | bytes 196640 | tf_op jit(solution)/shard_map/while/body/eval_jaxpr/ppermute | solution.py:10
  56.6 7.5 %collective-permute-start.1 = (bf16[768,128]{1,0:T(8,128)(2,1)S(1)}, bf16[768,128]{1,0:T(8,128)(2,1)S(1)}, u32[]{:S(2)}, u32[]{:S(2)}) collective-permute-start(bf16[768,128]{1,0:T(8,128)(2,1)S(1)} %copy.19), channel_id=1, source_target_pairs={{1,0},{2,1},{3,2},{4,3},{5,4},{6,5},{7,6},{9,8},{10,9},{11,10},{12... | collective-permute-start | bytes 589832 | tf_op jit(solution)/shard_map/while/body/eval_jaxpr/ppermute | solution.py:10
  64.2 3.2 %collective-permute-done.1 = bf16[768,128]{1,0:T(8,128)(2,1)S(1)} collective-permute-done((bf16[768,128]{1,0:T(8,128)(2,1)S(1)}, bf16[768,128]{1,0:T(8,128)(2,1)S(1)}, u32[]{:S(2)}, u32[]{:S(2)}) %collective-permute-start.1) | collective-permute-done | bytes 196640 | tf_op jit(solution)/shard_map/while/body/eval_jaxpr/ppermute | solution.py:10
  67.5 3.8 %collective-permute-start.1 = (bf16[768,128]{1,0:T(8,128)(2,1)S(1)}, bf16[768,128]{1,0:T(8,128)(2,1)S(1)}, u32[]{:S(2)}, u32[]{:S(2)}) collective-permute-start(bf16[768,128]{1,0:T(8,128)(2,1)S(1)} %copy.19), channel_id=1, source_target_pairs={{1,0},{2,1},{3,2},{4,3},{5,4},{6,5},{7,6},{9,8},{10,9},{11,10},{12... | collective-permute-start | bytes 589832 | tf_op jit(solution)/shard_map/while/body/eval_jaxpr/ppermute | solution.py:10
  71.3 3.2 %collective-permute-done.1 = bf16[768,128]{1,0:T(8,128)(2,1)S(1)} collective-permute-done((bf16[768,128]{1,0:T(8,128)(2,1)S(1)}, bf16[768,128]{1,0:T(8,128)(2,1)S(1)}, u32[]{:S(2)}, u32[]{:S(2)}) %collective-permute-start.1) | collective-permute-done | bytes 196640 | tf_op jit(solution)/shard_map/while/body/eval_jaxpr/ppermute | solution.py:10
  74.7 3.8 %collective-permute-start.1 = (bf16[768,128]{1,0:T(8,128)(2,1)S(1)}, bf16[768,128]{1,0:T(8,128)(2,1)S(1)}, u32[]{:S(2)}, u32[]{:S(2)}) collective-permute-start(bf16[768,128]{1,0:T(8,128)(2,1)S(1)} %copy.19), channel_id=1, source_target_pairs={{1,0},{2,1},{3,2},{4,3},{5,4},{6,5},{7,6},{9,8},{10,9},{11,10},{12... | collective-permute-start | bytes 589832 | tf_op jit(solution)/shard_map/while/body/eval_jaxpr/ppermute | solution.py:10
  78.5 3.2 %collective-permute-done.1 = bf16[768,128]{1,0:T(8,128)(2,1)S(1)} collective-permute-done((bf16[768,128]{1,0:T(8,128)(2,1)S(1)}, bf16[768,128]{1,0:T(8,128)(2,1)S(1)}, u32[]{:S(2)}, u32[]{:S(2)}) %collective-permute-start.1) | collective-permute-done | bytes 196640 | tf_op jit(solution)/shard_map/while/body/eval_jaxpr/ppermute | solution.py:10
  81.8 3.8 %collective-permute-start.1 = (bf16[768,128]{1,0:T(8,128)(2,1)S(1)}, bf16[768,128]{1,0:T(8,128)(2,1)S(1)}, u32[]{:S(2)}, u32[]{:S(2)}) collective-permute-start(bf16[768,128]{1,0:T(8,128)(2,1)S(1)} %copy.19), channel_id=1, source_target_pairs={{1,0},{2,1},{3,2},{4,3},{5,4},{6,5},{7,6},{9,8},{10,9},{11,10},{12... | collective-permute-start | bytes 589832 | tf_op jit(solution)/shard_map/while/body/eval_jaxpr/ppermute | solution.py:10
  85.6 3.2 %collective-permute-done.1 = bf16[768,128]{1,0:T(8,128)(2,1)S(1)} collective-permute-done((bf16[768,128]{1,0:T(8,128)(2,1)S(1)}, bf16[768,128]{1,0:T(8,128)(2,1)S(1)}, u32[]{:S(2)}, u32[]{:S(2)}) %collective-permute-start.1) | collective-permute-done | bytes 196640 | tf_op jit(solution)/shard_map/while/body/eval_jaxpr/ppermute | solution.py:10
  89.0 3.8 %collective-permute-start.1 = (bf16[768,128]{1,0:T(8,128)(2,1)S(1)}, bf16[768,128]{1,0:T(8,128)(2,1)S(1)}, u32[]{:S(2)}, u32[]{:S(2)}) collective-permute-start(bf16[768,128]{1,0:T(8,128)(2,1)S(1)} %copy.19), channel_id=1, source_target_pairs={{1,0},{2,1},{3,2},{4,3},{5,4},{6,5},{7,6},{9,8},{10,9},{11,10},{12... | collective-permute-start | bytes 589832 | tf_op jit(solution)/shard_map/while/body/eval_jaxpr/ppermute | solution.py:10
  92.8 3.2 %collective-permute-done.1 = bf16[768,128]{1,0:T(8,128)(2,1)S(1)} collective-permute-done((bf16[768,128]{1,0:T(8,128)(2,1)S(1)}, bf16[768,128]{1,0:T(8,128)(2,1)S(1)}, u32[]{:S(2)}, u32[]{:S(2)}) %collective-permute-start.1) | collective-permute-done | bytes 196640 | tf_op jit(solution)/shard_map/while/body/eval_jaxpr/ppermute | solution.py:10
  96.0 107.6 %while.37 = (s32[]{:T(128)}, bf16[768,128]{0,1:T(8,128)(2,1)S(1)}, f32[1,768]{1,0:T(1,128)S(1)}, s32[]{:T(128)}, pred[]{:T(512)}, /*index=5*/bf16[768,128]{1,0:T...) while((s32[]{:T(128)}, bf16[768,128]{0,1:T(8,128)(2,1)S(1)}, ...), condition=%wide.region_9.10_spmd.clone.clone, body=%wide.region_3.9_spmd.clone.clone.sunk | while | flops 302690304 | bytes 4156900 | solution.py:115
  96.2 1.9 collective-permute-start
  98.1 5.2 %collective-permute-done = bf16[768,128]{1,0:T(8,128)(2,1)S(1)} collective-permute-done((bf16[768,128]{1,0:T(8,128)(2,1)S(1)}, bf16[768,128]{1,0:T(8,128)(2,1)S(1)}, u32[]{:S(2)}, u32[]{:S(2)}) %collective-permute-start) | collective-permute-done | bytes 196640 | tf_op jit(solution)/shard_map/while/body/eval_jaxpr/ppermute | solution.py:10
  103.5 1.9 collective-permute-start
  105.4 5.0 %collective-permute-done = bf16[768,128]{1,0:T(8,128)(2,1)S(1)} collective-permute-done((bf16[768,128]{1,0:T(8,128)(2,1)S(1)}, bf16[768,128]{1,0:T(8,128)(2,1)S(1)}, u32[]{:S(2)}, u32[]{:S(2)}) %collective-permute-start) | collective-permute-done | bytes 196640 | tf_op jit(solution)/shard_map/while/body/eval_jaxpr/ppermute | solution.py:10
  110.7 1.9 collective-permute-start
  112.6 5.0 %collective-permute-done = bf16[768,128]{1,0:T(8,128)(2,1)S(1)} collective-permute-done((bf16[768,128]{1,0:T(8,128)(2,1)S(1)}, bf16[768,128]{1,0:T(8,128)(2,1)S(1)}, u32[]{:S(2)}, u32[]{:S(2)}) %collective-permute-start) | collective-permute-done | bytes 196640 | tf_op jit(solution)/shard_map/while/body/eval_jaxpr/ppermute | solution.py:10
  117.8 1.9 collective-permute-start
  119.8 5.0 %collective-permute-done = bf16[768,128]{1,0:T(8,128)(2,1)S(1)} collective-permute-done((bf16[768,128]{1,0:T(8,128)(2,1)S(1)}, bf16[768,128]{1,0:T(8,128)(2,1)S(1)}, u32[]{:S(2)}, u32[]{:S(2)}) %collective-permute-start) | collective-permute-done | bytes 196640 | tf_op jit(solution)/shard_map/while/body/eval_jaxpr/ppermute | solution.py:10
  125.0 1.9 collective-permute-start
  126.9 5.0 %collective-permute-done = bf16[768,128]{1,0:T(8,128)(2,1)S(1)} collective-permute-done((bf16[768,128]{1,0:T(8,128)(2,1)S(1)}, bf16[768,128]{1,0:T(8,128)(2,1)S(1)}, u32[]{:S(2)}, u32[]{:S(2)}) %collective-permute-start) | collective-permute-done | bytes 196640 | tf_op jit(solution)/shard_map/while/body/eval_jaxpr/ppermute | solution.py:10
  132.1 1.9 collective-permute-start
  134.1 5.0 %collective-permute-done = bf16[768,128]{1,0:T(8,128)(2,1)S(1)} collective-permute-done((bf16[768,128]{1,0:T(8,128)(2,1)S(1)}, bf16[768,128]{1,0:T(8,128)(2,1)S(1)}, u32[]{:S(2)}, u32[]{:S(2)}) %collective-permute-start) | collective-permute-done | bytes 196640 | tf_op jit(solution)/shard_map/while/body/eval_jaxpr/ppermute | solution.py:10
  139.3 1.9 collective-permute-start
  141.2 18.0 %collective-permute-done = bf16[768,128]{1,0:T(8,128)(2,1)S(1)} collective-permute-done((bf16[768,128]{1,0:T(8,128)(2,1)S(1)}, bf16[768,128]{1,0:T(8,128)(2,1)S(1)}, u32[]{:S(2)}, u32[]{:S(2)}) %collective-permute-start) | collective-permute-done | bytes 196640 | tf_op jit(solution)/shard_map/while/body/eval_jaxpr/ppermute | solution.py:10
  159.3 3.9 %conditional.8 = ((bf16[768,128]{0,1:T(8,128)(2,1)S(1)}, f32[1,768]{1,0:T(1,128)S(1)})) conditional(s32[]{:T(128)} %convert_element_type.148, (bf16[768,128]{0,1:T(8,128)(2,1)S(1)}, f32[1,768]{1,0:T(1,128)S(1)}) %tuple.125, (s32[4]{0:T(128)S(1)}, pred[]{:T(512)}, bf16[768,128]{1,0:T(8,128)(2,1)S(1)}, bf16[768,128]{1,0:T(8,128)(2,1)S(1)}, ...), branch_computations={%region_4.4_spmd, %region_5.8_spmd.clone} | conditional | flops 302690304 | bytes 2976905 | solution.py:84
  159.4 2.5 %multiply_reduce_fusion = (f32[768]{0:T(1024)S(1)}, bf16[768,128]{0,1:T(8,128)(2,1)S(1)}) fusion(bf16[1,768,768]{2,1,0:T(8,128)(2,1)} %get-tuple-element.827, bf16[1,768,768]{2,1,0:T(8,128)(2,1)} %get-tuple-element.826, bf16[768,128]{1,0:T(8,128)(2,1)S(1)} %get-tuple-element.824, bf16[768,128]{1,0:T(8,128)(2,1)S(1)} %get-tuple-element.825, ...), kind=kOutput, calls=%fused_computation.11 | convolution fusion | flops 302677248 | bytes 2955265 | tf_op jit(solution)/shard_map/while/body/eval_jaxpr/cond/branch_1_fun/dot_general | solution.py:52
  163.3 1.9 collective-permute-start
  165.3 5.1 %collective-permute-done = bf16[768,128]{1,0:T(8,128)(2,1)S(1)} collective-permute-done((bf16[768,128]{1,0:T(8,128)(2,1)S(1)}, bf16[768,128]{1,0:T(8,128)(2,1)S(1)}, u32[]{:S(2)}, u32[]{:S(2)}) %collective-permute-start) | collective-permute-done | bytes 196640 | tf_op jit(solution)/shard_map/while/body/eval_jaxpr/ppermute | solution.py:10
  170.3 3.9 %conditional.8 = ((bf16[768,128]{0,1:T(8,128)(2,1)S(1)}, f32[1,768]{1,0:T(1,128)S(1)})) conditional(s32[]{:T(128)} %convert_element_type.148, (bf16[768,128]{0,1:T(8,128)(2,1)S(1)}, f32[1,768]{1,0:T(1,128)S(1)}) %tuple.125, (s32[4]{0:T(128)S(1)}, pred[]{:T(512)}, bf16[768,128]{1,0:T(8,128)(2,1)S(1)}, bf16[768,128]{1,0:T(8,128)(2,1)S(1)}, ...), branch_computations={%region_4.4_spmd, %region_5.8_spmd.clone} | conditional | flops 302690304 | bytes 2976905 | solution.py:84
  170.4 2.5 %multiply_reduce_fusion = (f32[768]{0:T(1024)S(1)}, bf16[768,128]{0,1:T(8,128)(2,1)S(1)}) fusion(bf16[1,768,768]{2,1,0:T(8,128)(2,1)} %get-tuple-element.827, bf16[1,768,768]{2,1,0:T(8,128)(2,1)} %get-tuple-element.826, bf16[768,128]{1,0:T(8,128)(2,1)S(1)} %get-tuple-element.824, bf16[768,128]{1,0:T(8,128)(2,1)S(1)} %get-tuple-element.825, ...), kind=kOutput, calls=%fused_computation.11 | convolution fusion | flops 302677248 | bytes 2955265 | tf_op jit(solution)/shard_map/while/body/eval_jaxpr/cond/branch_1_fun/dot_general | solution.py:52
  174.4 1.9 collective-permute-start
  176.4 5.0 %collective-permute-done = bf16[768,128]{1,0:T(8,128)(2,1)S(1)} collective-permute-done((bf16[768,128]{1,0:T(8,128)(2,1)S(1)}, bf16[768,128]{1,0:T(8,128)(2,1)S(1)}, u32[]{:S(2)}, u32[]{:S(2)}) %collective-permute-start) | collective-permute-done | bytes 196640 | tf_op jit(solution)/shard_map/while/body/eval_jaxpr/ppermute | solution.py:10
  181.4 3.9 %conditional.8 = ((bf16[768,128]{0,1:T(8,128)(2,1)S(1)}, f32[1,768]{1,0:T(1,128)S(1)})) conditional(s32[]{:T(128)} %convert_element_type.148, (bf16[768,128]{0,1:T(8,128)(2,1)S(1)}, f32[1,768]{1,0:T(1,128)S(1)}) %tuple.125, (s32[4]{0:T(128)S(1)}, pred[]{:T(512)}, bf16[768,128]{1,0:T(8,128)(2,1)S(1)}, bf16[768,128]{1,0:T(8,128)(2,1)S(1)}, ...), branch_computations={%region_4.4_spmd, %region_5.8_spmd.clone} | conditional | flops 302690304 | bytes 2976905 | solution.py:84
  181.5 2.5 %multiply_reduce_fusion = (f32[768]{0:T(1024)S(1)}, bf16[768,128]{0,1:T(8,128)(2,1)S(1)}) fusion(bf16[1,768,768]{2,1,0:T(8,128)(2,1)} %get-tuple-element.827, bf16[1,768,768]{2,1,0:T(8,128)(2,1)} %get-tuple-element.826, bf16[768,128]{1,0:T(8,128)(2,1)S(1)} %get-tuple-element.824, bf16[768,128]{1,0:T(8,128)(2,1)S(1)} %get-tuple-element.825, ...), kind=kOutput, calls=%fused_computation.11 | convolution fusion | flops 302677248 | bytes 2955265 | tf_op jit(solution)/shard_map/while/body/eval_jaxpr/cond/branch_1_fun/dot_general | solution.py:52
  185.5 1.9 collective-permute-start
  187.4 5.0 %collective-permute-done = bf16[768,128]{1,0:T(8,128)(2,1)S(1)} collective-permute-done((bf16[768,128]{1,0:T(8,128)(2,1)S(1)}, bf16[768,128]{1,0:T(8,128)(2,1)S(1)}, u32[]{:S(2)}, u32[]{:S(2)}) %collective-permute-start) | collective-permute-done | bytes 196640 | tf_op jit(solution)/shard_map/while/body/eval_jaxpr/ppermute | solution.py:10
  192.5 3.9 %conditional.8 = ((bf16[768,128]{0,1:T(8,128)(2,1)S(1)}, f32[1,768]{1,0:T(1,128)S(1)})) conditional(s32[]{:T(128)} %convert_element_type.148, (bf16[768,128]{0,1:T(8,128)(2,1)S(1)}, f32[1,768]{1,0:T(1,128)S(1)}) %tuple.125, (s32[4]{0:T(128)S(1)}, pred[]{:T(512)}, bf16[768,128]{1,0:T(8,128)(2,1)S(1)}, bf16[768,128]{1,0:T(8,128)(2,1)S(1)}, ...), branch_computations={%region_4.4_spmd, %region_5.8_spmd.clone} | conditional | flops 302690304 | bytes 2976905 | solution.py:84
  192.6 2.5 %multiply_reduce_fusion = (f32[768]{0:T(1024)S(1)}, bf16[768,128]{0,1:T(8,128)(2,1)S(1)}) fusion(bf16[1,768,768]{2,1,0:T(8,128)(2,1)} %get-tuple-element.827, bf16[1,768,768]{2,1,0:T(8,128)(2,1)} %get-tuple-element.826, bf16[768,128]{1,0:T(8,128)(2,1)S(1)} %get-tuple-element.824, bf16[768,128]{1,0:T(8,128)(2,1)S(1)} %get-tuple-element.825, ...), kind=kOutput, calls=%fused_computation.11 | convolution fusion | flops 302677248 | bytes 2955265 | tf_op jit(solution)/shard_map/while/body/eval_jaxpr/cond/branch_1_fun/dot_general | solution.py:52
  196.6 1.9 collective-permute-start
  198.5 5.0 %collective-permute-done = bf16[768,128]{1,0:T(8,128)(2,1)S(1)} collective-permute-done((bf16[768,128]{1,0:T(8,128)(2,1)S(1)}, bf16[768,128]{1,0:T(8,128)(2,1)S(1)}, u32[]{:S(2)}, u32[]{:S(2)}) %collective-permute-start) | collective-permute-done | bytes 196640 | tf_op jit(solution)/shard_map/while/body/eval_jaxpr/ppermute | solution.py:10
  203.6 8.2 %all-gather.1 = f32[4,1,768]{2,1,0:T(1,128)S(1)} all-gather(f32[1,1,768]{2,1,0:T(1,128)S(1)} %add_bitcast_fusion), channel_id=2, replica_groups=mesh['energy'=4,'slab'=8] {'energy'}, dimensions={0}, use_global_device_ids=true | all-gather | bytes 15360 | tf_op jit(solution)/shard_map/all_gather | solution.py:117
  (110 shorter events, 15.8 us)
Async XLA Ops:
  2.4 93.6 %copy-start = (bf16[768,128]{1,0:T(8,128)(2,1)S(1)}, bf16[768,128]{1,0:T(8,128)(2,1)}, u32[]{:S(2)}) copy-start(bf16[768,128]{1,0:T(8,128)(2,1)} %param.24) | copy-start | bytes 589828
  2.6 5.1 %collective-permute-start.1 = (bf16[768,128]{1,0:T(8,128)(2,1)S(1)}, bf16[768,128]{1,0:T(8,128)(2,1)S(1)}, u32[]{:S(2)}, u32[]{:S(2)}) collective-permute-start(bf16[768,128]{1,0:T(8,128)(2,1)S(1)} %copy.19), channel_id=1, source_target_pairs={{1,0},{2,1},{3,2},{4,3},{5,4},{6,5},{7,6},{9,8},{10,9},{11,10},{12... | collective-permute-start | bytes 589832 | tf_op jit(solution)/shard_map/while/body/eval_jaxpr/ppermute | solution.py:10
  7.9 7.0 %collective-permute-start.1 = (bf16[768,128]{1,0:T(8,128)(2,1)S(1)}, bf16[768,128]{1,0:T(8,128)(2,1)S(1)}, u32[]{:S(2)}, u32[]{:S(2)}) collective-permute-start(bf16[768,128]{1,0:T(8,128)(2,1)S(1)} %copy.19), channel_id=1, source_target_pairs={{1,0},{2,1},{3,2},{4,3},{5,4},{6,5},{7,6},{9,8},{10,9},{11,10},{12... | collective-permute-start | bytes 589832 | tf_op jit(solution)/shard_map/while/body/eval_jaxpr/ppermute | solution.py:10
  18.8 5.1 %collective-permute-start.1 = (bf16[768,128]{1,0:T(8,128)(2,1)S(1)}, bf16[768,128]{1,0:T(8,128)(2,1)S(1)}, u32[]{:S(2)}, u32[]{:S(2)}) collective-permute-start(bf16[768,128]{1,0:T(8,128)(2,1)S(1)} %copy.19), channel_id=1, source_target_pairs={{1,0},{2,1},{3,2},{4,3},{5,4},{6,5},{7,6},{9,8},{10,9},{11,10},{12... | collective-permute-start | bytes 589832 | tf_op jit(solution)/shard_map/while/body/eval_jaxpr/ppermute | solution.py:10
  27.7 7.0 %collective-permute-start.1 = (bf16[768,128]{1,0:T(8,128)(2,1)S(1)}, bf16[768,128]{1,0:T(8,128)(2,1)S(1)}, u32[]{:S(2)}, u32[]{:S(2)}) collective-permute-start(bf16[768,128]{1,0:T(8,128)(2,1)S(1)} %copy.19), channel_id=1, source_target_pairs={{1,0},{2,1},{3,2},{4,3},{5,4},{6,5},{7,6},{9,8},{10,9},{11,10},{12... | collective-permute-start | bytes 589832 | tf_op jit(solution)/shard_map/while/body/eval_jaxpr/ppermute | solution.py:10
  38.6 7.0 %collective-permute-start.1 = (bf16[768,128]{1,0:T(8,128)(2,1)S(1)}, bf16[768,128]{1,0:T(8,128)(2,1)S(1)}, u32[]{:S(2)}, u32[]{:S(2)}) collective-permute-start(bf16[768,128]{1,0:T(8,128)(2,1)S(1)} %copy.19), channel_id=1, source_target_pairs={{1,0},{2,1},{3,2},{4,3},{5,4},{6,5},{7,6},{9,8},{10,9},{11,10},{12... | collective-permute-start | bytes 589832 | tf_op jit(solution)/shard_map/while/body/eval_jaxpr/ppermute | solution.py:10
  49.5 7.0 %collective-permute-start.1 = (bf16[768,128]{1,0:T(8,128)(2,1)S(1)}, bf16[768,128]{1,0:T(8,128)(2,1)S(1)}, u32[]{:S(2)}, u32[]{:S(2)}) collective-permute-start(bf16[768,128]{1,0:T(8,128)(2,1)S(1)} %copy.19), channel_id=1, source_target_pairs={{1,0},{2,1},{3,2},{4,3},{5,4},{6,5},{7,6},{9,8},{10,9},{11,10},{12... | collective-permute-start | bytes 589832 | tf_op jit(solution)/shard_map/while/body/eval_jaxpr/ppermute | solution.py:10
  56.6 10.7 %collective-permute-start.1 = (bf16[768,128]{1,0:T(8,128)(2,1)S(1)}, bf16[768,128]{1,0:T(8,128)(2,1)S(1)}, u32[]{:S(2)}, u32[]{:S(2)}) collective-permute-start(bf16[768,128]{1,0:T(8,128)(2,1)S(1)} %copy.19), channel_id=1, source_target_pairs={{1,0},{2,1},{3,2},{4,3},{5,4},{6,5},{7,6},{9,8},{10,9},{11,10},{12... | collective-permute-start | bytes 589832 | tf_op jit(solution)/shard_map/while/body/eval_jaxpr/ppermute | solution.py:10
  67.5 7.0 %collective-permute-start.1 = (bf16[768,128]{1,0:T(8,128)(2,1)S(1)}, bf16[768,128]{1,0:T(8,128)(2,1)S(1)}, u32[]{:S(2)}, u32[]{:S(2)}) collective-permute-start(bf16[768,128]{1,0:T(8,128)(2,1)S(1)} %copy.19), channel_id=1, source_target_pairs={{1,0},{2,1},{3,2},{4,3},{5,4},{6,5},{7,6},{9,8},{10,9},{11,10},{12... | collective-permute-start | bytes 589832 | tf_op jit(solution)/shard_map/while/body/eval_jaxpr/ppermute | solution.py:10
  74.7 7.0 %collective-permute-start.1 = (bf16[768,128]{1,0:T(8,128)(2,1)S(1)}, bf16[768,128]{1,0:T(8,128)(2,1)S(1)}, u32[]{:S(2)}, u32[]{:S(2)}) collective-permute-start(bf16[768,128]{1,0:T(8,128)(2,1)S(1)} %copy.19), channel_id=1, source_target_pairs={{1,0},{2,1},{3,2},{4,3},{5,4},{6,5},{7,6},{9,8},{10,9},{11,10},{12... | collective-permute-start | bytes 589832 | tf_op jit(solution)/shard_map/while/body/eval_jaxpr/ppermute | solution.py:10
  81.8 7.0 %collective-permute-start.1 = (bf16[768,128]{1,0:T(8,128)(2,1)S(1)}, bf16[768,128]{1,0:T(8,128)(2,1)S(1)}, u32[]{:S(2)}, u32[]{:S(2)}) collective-permute-start(bf16[768,128]{1,0:T(8,128)(2,1)S(1)} %copy.19), channel_id=1, source_target_pairs={{1,0},{2,1},{3,2},{4,3},{5,4},{6,5},{7,6},{9,8},{10,9},{11,10},{12... | collective-permute-start | bytes 589832 | tf_op jit(solution)/shard_map/while/body/eval_jaxpr/ppermute | solution.py:10
  89.0 7.0 %collective-permute-start.1 = (bf16[768,128]{1,0:T(8,128)(2,1)S(1)}, bf16[768,128]{1,0:T(8,128)(2,1)S(1)}, u32[]{:S(2)}, u32[]{:S(2)}) collective-permute-start(bf16[768,128]{1,0:T(8,128)(2,1)S(1)} %copy.19), channel_id=1, source_target_pairs={{1,0},{2,1},{3,2},{4,3},{5,4},{6,5},{7,6},{9,8},{10,9},{11,10},{12... | collective-permute-start | bytes 589832 | tf_op jit(solution)/shard_map/while/body/eval_jaxpr/ppermute | solution.py:10
  96.2 7.2 %collective-permute-start = (bf16[768,128]{1,0:T(8,128)(2,1)S(1)}, bf16[768,128]{1,0:T(8,128)(2,1)S(1)}, u32[]{:S(2)}, u32[]{:S(2)}) collective-permute-start(bf16[768,128]{1,0:T(8,128)(2,1)S(1)} %copy.18), channel_id=1, source_target_pairs={{0,1},{1,2},{2,3},{3,4},{4,5},{5,6},{6,7},{8,9},{9,10},{10,11},{11... | collective-permute-start | bytes 589832 | tf_op jit(solution)/shard_map/while/body/eval_jaxpr/ppermute | solution.py:10
  103.5 7.0 %collective-permute-start = (bf16[768,128]{1,0:T(8,128)(2,1)S(1)}, bf16[768,128]{1,0:T(8,128)(2,1)S(1)}, u32[]{:S(2)}, u32[]{:S(2)}) collective-permute-start(bf16[768,128]{1,0:T(8,128)(2,1)S(1)} %copy.18), channel_id=1, source_target_pairs={{0,1},{1,2},{2,3},{3,4},{4,5},{5,6},{6,7},{8,9},{9,10},{10,11},{11... | collective-permute-start | bytes 589832 | tf_op jit(solution)/shard_map/while/body/eval_jaxpr/ppermute | solution.py:10
  110.7 7.0 %collective-permute-start = (bf16[768,128]{1,0:T(8,128)(2,1)S(1)}, bf16[768,128]{1,0:T(8,128)(2,1)S(1)}, u32[]{:S(2)}, u32[]{:S(2)}) collective-permute-start(bf16[768,128]{1,0:T(8,128)(2,1)S(1)} %copy.18), channel_id=1, source_target_pairs={{0,1},{1,2},{2,3},{3,4},{4,5},{5,6},{6,7},{8,9},{9,10},{10,11},{11... | collective-permute-start | bytes 589832 | tf_op jit(solution)/shard_map/while/body/eval_jaxpr/ppermute | solution.py:10
  117.8 7.0 %collective-permute-start = (bf16[768,128]{1,0:T(8,128)(2,1)S(1)}, bf16[768,128]{1,0:T(8,128)(2,1)S(1)}, u32[]{:S(2)}, u32[]{:S(2)}) collective-permute-start(bf16[768,128]{1,0:T(8,128)(2,1)S(1)} %copy.18), channel_id=1, source_target_pairs={{0,1},{1,2},{2,3},{3,4},{4,5},{5,6},{6,7},{8,9},{9,10},{10,11},{11... | collective-permute-start | bytes 589832 | tf_op jit(solution)/shard_map/while/body/eval_jaxpr/ppermute | solution.py:10
  125.0 7.0 %collective-permute-start = (bf16[768,128]{1,0:T(8,128)(2,1)S(1)}, bf16[768,128]{1,0:T(8,128)(2,1)S(1)}, u32[]{:S(2)}, u32[]{:S(2)}) collective-permute-start(bf16[768,128]{1,0:T(8,128)(2,1)S(1)} %copy.18), channel_id=1, source_target_pairs={{0,1},{1,2},{2,3},{3,4},{4,5},{5,6},{6,7},{8,9},{9,10},{10,11},{11... | collective-permute-start | bytes 589832 | tf_op jit(solution)/shard_map/while/body/eval_jaxpr/ppermute | solution.py:10
  132.1 7.0 %collective-permute-start = (bf16[768,128]{1,0:T(8,128)(2,1)S(1)}, bf16[768,128]{1,0:T(8,128)(2,1)S(1)}, u32[]{:S(2)}, u32[]{:S(2)}) collective-permute-start(bf16[768,128]{1,0:T(8,128)(2,1)S(1)} %copy.18), channel_id=1, source_target_pairs={{0,1},{1,2},{2,3},{3,4},{4,5},{5,6},{6,7},{8,9},{9,10},{10,11},{11... | collective-permute-start | bytes 589832 | tf_op jit(solution)/shard_map/while/body/eval_jaxpr/ppermute | solution.py:10
  139.3 20.0 %collective-permute-start = (bf16[768,128]{1,0:T(8,128)(2,1)S(1)}, bf16[768,128]{1,0:T(8,128)(2,1)S(1)}, u32[]{:S(2)}, u32[]{:S(2)}) collective-permute-start(bf16[768,128]{1,0:T(8,128)(2,1)S(1)} %copy.18), channel_id=1, source_target_pairs={{0,1},{1,2},{2,3},{3,4},{4,5},{5,6},{6,7},{8,9},{9,10},{10,11},{11... | collective-permute-start | bytes 589832 | tf_op jit(solution)/shard_map/while/body/eval_jaxpr/ppermute | solution.py:10
  163.3 7.0 %collective-permute-start = (bf16[768,128]{1,0:T(8,128)(2,1)S(1)}, bf16[768,128]{1,0:T(8,128)(2,1)S(1)}, u32[]{:S(2)}, u32[]{:S(2)}) collective-permute-start(bf16[768,128]{1,0:T(8,128)(2,1)S(1)} %copy.18), channel_id=1, source_target_pairs={{0,1},{1,2},{2,3},{3,4},{4,5},{5,6},{6,7},{8,9},{9,10},{10,11},{11... | collective-permute-start | bytes 589832 | tf_op jit(solution)/shard_map/while/body/eval_jaxpr/ppermute | solution.py:10
  174.4 7.0 %collective-permute-start = (bf16[768,128]{1,0:T(8,128)(2,1)S(1)}, bf16[768,128]{1,0:T(8,128)(2,1)S(1)}, u32[]{:S(2)}, u32[]{:S(2)}) collective-permute-start(bf16[768,128]{1,0:T(8,128)(2,1)S(1)} %copy.18), channel_id=1, source_target_pairs={{0,1},{1,2},{2,3},{3,4},{4,5},{5,6},{6,7},{8,9},{9,10},{10,11},{11... | collective-permute-start | bytes 589832 | tf_op jit(solution)/shard_map/while/body/eval_jaxpr/ppermute | solution.py:10
  185.5 7.0 %collective-permute-start = (bf16[768,128]{1,0:T(8,128)(2,1)S(1)}, bf16[768,128]{1,0:T(8,128)(2,1)S(1)}, u32[]{:S(2)}, u32[]{:S(2)}) collective-permute-start(bf16[768,128]{1,0:T(8,128)(2,1)S(1)} %copy.18), channel_id=1, source_target_pairs={{0,1},{1,2},{2,3},{3,4},{4,5},{5,6},{6,7},{8,9},{9,10},{10,11},{11... | collective-permute-start | bytes 589832 | tf_op jit(solution)/shard_map/while/body/eval_jaxpr/ppermute | solution.py:10
  196.6 7.0 %collective-permute-start = (bf16[768,128]{1,0:T(8,128)(2,1)S(1)}, bf16[768,128]{1,0:T(8,128)(2,1)S(1)}, u32[]{:S(2)}, u32[]{:S(2)}) collective-permute-start(bf16[768,128]{1,0:T(8,128)(2,1)S(1)} %copy.18), channel_id=1, source_target_pairs={{0,1},{1,2},{2,3},{3,4},{4,5},{5,6},{6,7},{8,9},{9,10},{10,11},{11... | collective-permute-start | bytes 589832 | tf_op jit(solution)/shard_map/while/body/eval_jaxpr/ppermute | solution.py:10
